TPU v7x, 512 devices: a whole 4x8x8 slice. The times are simulated.
512 devices in a mesh: src: 16 (over z, x_lo), xl: 32 (over y, x_hi, core).
Axes of the slice: x: 4 (x_hi: 2, x_lo: 2; x = x_hi * 2 + x_lo), y: 8, z: 8, core: 2. Of those that a mesh axis runs over, the one named last changes fastest.
Arguments:
- src_traces: float32 [256, 1024, 1024], P('src', 'xl'), may hold values from -6 to 6
- rec_traces: float32 [1024, 256, 1024], P('xl', 'src'), may hold values from -6 to 6
Outputs:
- multiples: float32 [256, 256, 256], P('src', 'xl')
All inputs are finite; a program needn't handle non-finite values.
Results may differ from a plain program's by a relative error of at most 0.004.
Values may be sent and summed in bfloat16 or wider, within the bound.
A program may use at most 64 MiB of HBM per device.

v0:
```python
import math

import jax
import jax.numpy as jnp
from jax import lax
from jax.sharding import PartitionSpec as P

F = 128
FBASE = 4


def from_behind(value, axis, steps):
    count = lax.axis_size(axis)
    pairs = [(source, (source + steps) % count) for source in range(count)]
    return lax.ppermute(value, axis, pairs)


def fourier_table(samples):
    times = jnp.arange(samples, dtype=jnp.int32)
    freq_bins = FBASE + jnp.arange(F, dtype=jnp.int32)
    phases = times[:, None] * freq_bins[None, :] % samples
    angles = phases.astype(jnp.float32) * jnp.float32(2.0 * math.pi / samples)
    basis = jnp.concatenate([jnp.cos(angles), -jnp.sin(angles)], axis=1)
    return basis / jnp.float32(math.sqrt(samples))


def spectra(traces):
    samples = traces.shape[-1]
    flat_rows = traces.reshape(-1, samples)
    result = jnp.dot(
        flat_rows,
        fourier_table(samples),
        precision=lax.Precision.HIGHEST,
        preferred_element_type=jnp.float32,
    )
    return result.reshape(traces.shape[:-1] + (2 * F,)).astype(jnp.bfloat16)


def spectral_product(left, right, layout_kind):
    left_re = left[..., :F]
    left_im = left[..., F:]
    right_re = right[..., :F]
    right_im = right[..., F:]
    real_part = jnp.einsum(
        layout_kind, left_re, right_re, preferred_element_type=jnp.float32
    ) - jnp.einsum(layout_kind, left_im, right_im, preferred_element_type=jnp.float32)
    imag_part = jnp.einsum(
        layout_kind, left_re, right_im, preferred_element_type=jnp.float32
    ) + jnp.einsum(layout_kind, left_im, right_re, preferred_element_type=jnp.float32)
    return jnp.concatenate([real_part, imag_part], axis=-1)


def per_device(src_traces, rec_traces):
    shot_source = spectra(src_traces)
    own_panels = spectra(rec_traces)
    members = lax.axis_size("xl")
    weighting_factor = jnp.float32(1.0 / math.sqrt(shot_source.shape[1] * members))
    panels = lax.all_gather(own_panels, "src", axis=1, tiled=True)
    panel_block_width = panels.shape[1] // members
    position = lax.axis_index("xl")

    def block_term(block):
        slice_portion = lax.dynamic_slice_in_dim(
            panels, block * panel_block_width, panel_block_width, 1
        )
        return spectral_product(shot_source, slice_portion, "ltu,teu->leu") * weighting_factor

    start_offset = block_term((position + members - 1) % members)

    def advance(section, carried):
        moved = from_behind(carried, "xl", 1)
        block = (position - section + members - 1) % members
        return moved + block_term(block)

    result = lax.fori_loop(1, members, advance, start_offset)
    return result


def solution(mesh):
    return jax.shard_map(
        per_device,
        mesh=mesh,
        in_specs=(P("src", "xl", None), P("xl", "src", None)),
        out_specs=P("src", "xl", None),
        check_vma=False,
    )
```

profile of v0, /device:TPU:1, one launch (start us, length us, event | category | flops | bytes accessed | tf_op | source)
XLA Modules:
  0.0 816.7 jit_solution(11534181868559429263)
XLA Ops:
  6.5 2.1 fusion.39
  8.6 4.3 fusion.19
  14.0 2.0 copy.15
  16.1 5.2 fusion.20
  21.4 1.9 copy.17
  23.3 348.8 %all-gather.2.cloned.1.call-done = bf16[32,256,256]{0,1,2:T(8,128)(2,1)} async-done(((bf16[32,16,256]{0,1,2:T(8,128)(2,1)}), bf16[32,256,256]{0,1,2:T(8,128)(2,1)}) %all-gather.2.cloned.1.call-update) | async-done | bytes 4194320 | tf_op jit(solution)/shard_map/all_gather | solution.py:58
  382.8 426.4 %while.17 = (s32[]{:T(128)}, f32[16,8,256]{2,1,0:T(8,128)S(1)}, s32[]{:T(128)}, bf16[32,256,256]{0,1,2:T(8,128)(2,1)}, bf16[16,32,256]{1,0,2:T(8,128)(2,1)}, /*i...) while((s32[]{:T(128)}, f32[16,8,256]{2,1,0:T(8,128)S(1)}, ...), condition=%wide.region_1.2_spmd, body=%wide.region_0.1_spmd.sunk | while | flops 4325395 | bytes 5243224 | solution.py:75
  382.8 9.7 %collective-permute-start = (f32[16,8,256]{2,1,0:T(8,128)S(1)}, f32[16,8,256]{2,1,0:T(8,128)S(1)}, u32[]{:S(2)}, u32[]{:S(2)}) collective-permute-start(f32[16,8,256]{2,1,0:T(8,128)S(1)} %get-tuple-element.243), channel_id=1, source_target_pairs={{0,1},{1,2},{2,3},{3,4},{4,5},{5,6},{6,7},{7,8},{8,9},{9,10},{10,1... | collective-permute-start | bytes 393224 | tf_op jit(solution)/shard_map/while/body/eval_jaxpr/ppermute | solution.py:15
  399.8 1.4 fusion.122
  403.1 1.9 collective-permute-start
  412.3 1.4 fusion.122
  415.6 3.5 collective-permute-start
  426.3 1.4 fusion.122
  429.7 1.9 collective-permute-start
  438.8 1.4 fusion.122
  442.2 5.0 collective-permute-start
  457.7 1.9 collective-permute-start
  466.9 1.4 fusion.122
  470.2 3.5 collective-permute-start
  481.0 1.4 fusion.122
  484.3 1.9 collective-permute-start
  493.5 1.4 fusion.122
  496.8 5.0 collective-permute-start
  509.1 1.4 fusion.122
  512.4 1.9 collective-permute-start
  521.6 1.4 fusion.122
  524.9 3.5 collective-permute-start
  539.0 1.9 collective-permute-start
  548.1 1.4 fusion.122
  551.5 5.0 collective-permute-start
  567.0 1.9 collective-permute-start
  579.5 4.7 collective-permute-start
  591.5 1.4 fusion.122
  594.8 1.9 collective-permute-start
  604.0 1.4 fusion.122
  607.3 5.0 collective-permute-start
  619.6 1.4 fusion.122
  622.9 1.9 collective-permute-start
  632.1 1.4 fusion.122
  635.4 2.6 collective-permute-start
  645.2 1.4 fusion.122
  648.6 1.9 collective-permute-start
  657.7 1.4 fusion.122
  661.1 5.0 collective-permute-start
  673.3 1.4 fusion.122
  676.7 1.9 collective-permute-start
  685.8 1.4 fusion.122
  689.2 2.6 collective-permute-start
  699.0 1.4 fusion.122
  702.3 1.9 collective-permute-start
  711.5 1.4 fusion.122
  714.8 5.0 collective-permute-start
  727.1 1.4 fusion.122
  730.4 1.9 collective-permute-start
  739.6 1.4 fusion.122
  742.9 2.6 collective-permute-start
  752.7 1.4 fusion.122
  756.1 1.9 collective-permute-start
  765.2 1.4 fusion.122
  768.6 5.0 collective-permute-start
  780.8 1.4 fusion.122
  784.1 1.9 collective-permute-start
  793.3 1.4 fusion.122
  796.7 1.9 collective-permute-start
  (366 shorter events, 300.4 us)
Async XLA Ops:
  6.5 2.1 copy-start
  6.5 365.6 %all-gather.2.cloned.1.call-start = ((), (), s32[]{:S(2)}) async-start(), calls=%async_computation | async-start | bytes 17825792 | tf_op jit(solution)/shard_map/all_gather | solution.py:58
  382.8 20.3 %collective-permute-start = (f32[16,8,256]{2,1,0:T(8,128)S(1)}, f32[16,8,256]{2,1,0:T(8,128)S(1)}, u32[]{:S(2)}, u32[]{:S(2)}) collective-permute-start(f32[16,8,256]{2,1,0:T(8,128)S(1)} %get-tuple-element.243), channel_id=1, source_target_pairs={{0,1},{1,2},{2,3},{3,4},{4,5},{5,6},{6,7},{7,8},{8,9},{9,10},{10,1... | collective-permute-start | bytes 393224 | tf_op jit(solution)/shard_map/while/body/eval_jaxpr/ppermute | solution.py:15
  403.1 12.5 %collective-permute-start = (f32[16,8,256]{2,1,0:T(8,128)S(1)}, f32[16,8,256]{2,1,0:T(8,128)S(1)}, u32[]{:S(2)}, u32[]{:S(2)}) collective-permute-start(f32[16,8,256]{2,1,0:T(8,128)S(1)} %get-tuple-element.243), channel_id=1, source_target_pairs={{0,1},{1,2},{2,3},{3,4},{4,5},{5,6},{6,7},{7,8},{8,9},{9,10},{10,1... | collective-permute-start | bytes 393224 | tf_op jit(solution)/shard_map/while/body/eval_jaxpr/ppermute | solution.py:15
  415.6 14.0 %collective-permute-start = (f32[16,8,256]{2,1,0:T(8,128)S(1)}, f32[16,8,256]{2,1,0:T(8,128)S(1)}, u32[]{:S(2)}, u32[]{:S(2)}) collective-permute-start(f32[16,8,256]{2,1,0:T(8,128)S(1)} %get-tuple-element.243), channel_id=1, source_target_pairs={{0,1},{1,2},{2,3},{3,4},{4,5},{5,6},{6,7},{7,8},{8,9},{9,10},{10,1... | collective-permute-start | bytes 393224 | tf_op jit(solution)/shard_map/while/body/eval_jaxpr/ppermute | solution.py:15
  429.7 12.5 %collective-permute-start = (f32[16,8,256]{2,1,0:T(8,128)S(1)}, f32[16,8,256]{2,1,0:T(8,128)S(1)}, u32[]{:S(2)}, u32[]{:S(2)}) collective-permute-start(f32[16,8,256]{2,1,0:T(8,128)S(1)} %get-tuple-element.243), channel_id=1, source_target_pairs={{0,1},{1,2},{2,3},{3,4},{4,5},{5,6},{6,7},{7,8},{8,9},{9,10},{10,1... | collective-permute-start | bytes 393224 | tf_op jit(solution)/shard_map/while/body/eval_jaxpr/ppermute | solution.py:15
  442.2 15.5 %collective-permute-start = (f32[16,8,256]{2,1,0:T(8,128)S(1)}, f32[16,8,256]{2,1,0:T(8,128)S(1)}, u32[]{:S(2)}, u32[]{:S(2)}) collective-permute-start(f32[16,8,256]{2,1,0:T(8,128)S(1)} %get-tuple-element.243), channel_id=1, source_target_pairs={{0,1},{1,2},{2,3},{3,4},{4,5},{5,6},{6,7},{7,8},{8,9},{9,10},{10,1... | collective-permute-start | bytes 393224 | tf_op jit(solution)/shard_map/while/body/eval_jaxpr/ppermute | solution.py:15
  457.7 12.5 %collective-permute-start = (f32[16,8,256]{2,1,0:T(8,128)S(1)}, f32[16,8,256]{2,1,0:T(8,128)S(1)}, u32[]{:S(2)}, u32[]{:S(2)}) collective-permute-start(f32[16,8,256]{2,1,0:T(8,128)S(1)} %get-tuple-element.243), channel_id=1, source_target_pairs={{0,1},{1,2},{2,3},{3,4},{4,5},{5,6},{6,7},{7,8},{8,9},{9,10},{10,1... | collective-permute-start | bytes 393224 | tf_op jit(solution)/shard_map/while/body/eval_jaxpr/ppermute | solution.py:15
  470.2 14.0 %collective-permute-start = (f32[16,8,256]{2,1,0:T(8,128)S(1)}, f32[16,8,256]{2,1,0:T(8,128)S(1)}, u32[]{:S(2)}, u32[]{:S(2)}) collective-permute-start(f32[16,8,256]{2,1,0:T(8,128)S(1)} %get-tuple-element.243), channel_id=1, source_target_pairs={{0,1},{1,2},{2,3},{3,4},{4,5},{5,6},{6,7},{7,8},{8,9},{9,10},{10,1... | collective-permute-start | bytes 393224 | tf_op jit(solution)/shard_map/while/body/eval_jaxpr/ppermute | solution.py:15
  484.3 12.5 %collective-permute-start = (f32[16,8,256]{2,1,0:T(8,128)S(1)}, f32[16,8,256]{2,1,0:T(8,128)S(1)}, u32[]{:S(2)}, u32[]{:S(2)}) collective-permute-start(f32[16,8,256]{2,1,0:T(8,128)S(1)} %get-tuple-element.243), channel_id=1, source_target_pairs={{0,1},{1,2},{2,3},{3,4},{4,5},{5,6},{6,7},{7,8},{8,9},{9,10},{10,1... | collective-permute-start | bytes 393224 | tf_op jit(solution)/shard_map/while/body/eval_jaxpr/ppermute | solution.py:15
  496.8 15.5 %collective-permute-start = (f32[16,8,256]{2,1,0:T(8,128)S(1)}, f32[16,8,256]{2,1,0:T(8,128)S(1)}, u32[]{:S(2)}, u32[]{:S(2)}) collective-permute-start(f32[16,8,256]{2,1,0:T(8,128)S(1)} %get-tuple-element.243), channel_id=1, source_target_pairs={{0,1},{1,2},{2,3},{3,4},{4,5},{5,6},{6,7},{7,8},{8,9},{9,10},{10,1... | collective-permute-start | bytes 393224 | tf_op jit(solution)/shard_map/while/body/eval_jaxpr/ppermute | solution.py:15
  512.4 12.5 %collective-permute-start = (f32[16,8,256]{2,1,0:T(8,128)S(1)}, f32[16,8,256]{2,1,0:T(8,128)S(1)}, u32[]{:S(2)}, u32[]{:S(2)}) collective-permute-start(f32[16,8,256]{2,1,0:T(8,128)S(1)} %get-tuple-element.243), channel_id=1, source_target_pairs={{0,1},{1,2},{2,3},{3,4},{4,5},{5,6},{6,7},{7,8},{8,9},{9,10},{10,1... | collective-permute-start | bytes 393224 | tf_op jit(solution)/shard_map/while/body/eval_jaxpr/ppermute | solution.py:15
  524.9 14.0 %collective-permute-start = (f32[16,8,256]{2,1,0:T(8,128)S(1)}, f32[16,8,256]{2,1,0:T(8,128)S(1)}, u32[]{:S(2)}, u32[]{:S(2)}) collective-permute-start(f32[16,8,256]{2,1,0:T(8,128)S(1)} %get-tuple-element.243), channel_id=1, source_target_pairs={{0,1},{1,2},{2,3},{3,4},{4,5},{5,6},{6,7},{7,8},{8,9},{9,10},{10,1... | collective-permute-start | bytes 393224 | tf_op jit(solution)/shard_map/while/body/eval_jaxpr/ppermute | solution.py:15
  539.0 12.5 %collective-permute-start = (f32[16,8,256]{2,1,0:T(8,128)S(1)}, f32[16,8,256]{2,1,0:T(8,128)S(1)}, u32[]{:S(2)}, u32[]{:S(2)}) collective-permute-start(f32[16,8,256]{2,1,0:T(8,128)S(1)} %get-tuple-element.243), channel_id=1, source_target_pairs={{0,1},{1,2},{2,3},{3,4},{4,5},{5,6},{6,7},{7,8},{8,9},{9,10},{10,1... | collective-permute-start | bytes 393224 | tf_op jit(solution)/shard_map/while/body/eval_jaxpr/ppermute | solution.py:15
  551.5 15.5 %collective-permute-start = (f32[16,8,256]{2,1,0:T(8,128)S(1)}, f32[16,8,256]{2,1,0:T(8,128)S(1)}, u32[]{:S(2)}, u32[]{:S(2)}) collective-permute-start(f32[16,8,256]{2,1,0:T(8,128)S(1)} %get-tuple-element.243), channel_id=1, source_target_pairs={{0,1},{1,2},{2,3},{3,4},{4,5},{5,6},{6,7},{7,8},{8,9},{9,10},{10,1... | collective-permute-start | bytes 393224 | tf_op jit(solution)/shard_map/while/body/eval_jaxpr/ppermute | solution.py:15
  567.0 12.5 %collective-permute-start = (f32[16,8,256]{2,1,0:T(8,128)S(1)}, f32[16,8,256]{2,1,0:T(8,128)S(1)}, u32[]{:S(2)}, u32[]{:S(2)}) collective-permute-start(f32[16,8,256]{2,1,0:T(8,128)S(1)} %get-tuple-element.243), channel_id=1, source_target_pairs={{0,1},{1,2},{2,3},{3,4},{4,5},{5,6},{6,7},{7,8},{8,9},{9,10},{10,1... | collective-permute-start | bytes 393224 | tf_op jit(solution)/shard_map/while/body/eval_jaxpr/ppermute | solution.py:15
  579.5 15.2 %collective-permute-start = (f32[16,8,256]{2,1,0:T(8,128)S(1)}, f32[16,8,256]{2,1,0:T(8,128)S(1)}, u32[]{:S(2)}, u32[]{:S(2)}) collective-permute-start(f32[16,8,256]{2,1,0:T(8,128)S(1)} %get-tuple-element.243), channel_id=1, source_target_pairs={{0,1},{1,2},{2,3},{3,4},{4,5},{5,6},{6,7},{7,8},{8,9},{9,10},{10,1... | collective-permute-start | bytes 393224 | tf_op jit(solution)/shard_map/while/body/eval_jaxpr/ppermute | solution.py:15
  594.8 12.5 %collective-permute-start = (f32[16,8,256]{2,1,0:T(8,128)S(1)}, f32[16,8,256]{2,1,0:T(8,128)S(1)}, u32[]{:S(2)}, u32[]{:S(2)}) collective-permute-start(f32[16,8,256]{2,1,0:T(8,128)S(1)} %get-tuple-element.243), channel_id=1, source_target_pairs={{0,1},{1,2},{2,3},{3,4},{4,5},{5,6},{6,7},{7,8},{8,9},{9,10},{10,1... | collective-permute-start | bytes 393224 | tf_op jit(solution)/shard_map/while/body/eval_jaxpr/ppermute | solution.py:15
  607.3 15.5 %collective-permute-start = (f32[16,8,256]{2,1,0:T(8,128)S(1)}, f32[16,8,256]{2,1,0:T(8,128)S(1)}, u32[]{:S(2)}, u32[]{:S(2)}) collective-permute-start(f32[16,8,256]{2,1,0:T(8,128)S(1)} %get-tuple-element.243), channel_id=1, source_target_pairs={{0,1},{1,2},{2,3},{3,4},{4,5},{5,6},{6,7},{7,8},{8,9},{9,10},{10,1... | collective-permute-start | bytes 393224 | tf_op jit(solution)/shard_map/while/body/eval_jaxpr/ppermute | solution.py:15
  622.9 12.5 %collective-permute-start = (f32[16,8,256]{2,1,0:T(8,128)S(1)}, f32[16,8,256]{2,1,0:T(8,128)S(1)}, u32[]{:S(2)}, u32[]{:S(2)}) collective-permute-start(f32[16,8,256]{2,1,0:T(8,128)S(1)} %get-tuple-element.243), channel_id=1, source_target_pairs={{0,1},{1,2},{2,3},{3,4},{4,5},{5,6},{6,7},{7,8},{8,9},{9,10},{10,1... | collective-permute-start | bytes 393224 | tf_op jit(solution)/shard_map/while/body/eval_jaxpr/ppermute | solution.py:15
  635.4 13.1 %collective-permute-start = (f32[16,8,256]{2,1,0:T(8,128)S(1)}, f32[16,8,256]{2,1,0:T(8,128)S(1)}, u32[]{:S(2)}, u32[]{:S(2)}) collective-permute-start(f32[16,8,256]{2,1,0:T(8,128)S(1)} %get-tuple-element.243), channel_id=1, source_target_pairs={{0,1},{1,2},{2,3},{3,4},{4,5},{5,6},{6,7},{7,8},{8,9},{9,10},{10,1... | collective-permute-start | bytes 393224 | tf_op jit(solution)/shard_map/while/body/eval_jaxpr/ppermute | solution.py:15
  648.6 12.5 %collective-permute-start = (f32[16,8,256]{2,1,0:T(8,128)S(1)}, f32[16,8,256]{2,1,0:T(8,128)S(1)}, u32[]{:S(2)}, u32[]{:S(2)}) collective-permute-start(f32[16,8,256]{2,1,0:T(8,128)S(1)} %get-tuple-element.243), channel_id=1, source_target_pairs={{0,1},{1,2},{2,3},{3,4},{4,5},{5,6},{6,7},{7,8},{8,9},{9,10},{10,1... | collective-permute-start | bytes 393224 | tf_op jit(solution)/shard_map/while/body/eval_jaxpr/ppermute | solution.py:15
  661.1 15.5 %collective-permute-start = (f32[16,8,256]{2,1,0:T(8,128)S(1)}, f32[16,8,256]{2,1,0:T(8,128)S(1)}, u32[]{:S(2)}, u32[]{:S(2)}) collective-permute-start(f32[16,8,256]{2,1,0:T(8,128)S(1)} %get-tuple-element.243), channel_id=1, source_target_pairs={{0,1},{1,2},{2,3},{3,4},{4,5},{5,6},{6,7},{7,8},{8,9},{9,10},{10,1... | collective-permute-start | bytes 393224 | tf_op jit(solution)/shard_map/while/body/eval_jaxpr/ppermute | solution.py:15
  676.7 12.5 %collective-permute-start = (f32[16,8,256]{2,1,0:T(8,128)S(1)}, f32[16,8,256]{2,1,0:T(8,128)S(1)}, u32[]{:S(2)}, u32[]{:S(2)}) collective-permute-start(f32[16,8,256]{2,1,0:T(8,128)S(1)} %get-tuple-element.243), channel_id=1, source_target_pairs={{0,1},{1,2},{2,3},{3,4},{4,5},{5,6},{6,7},{7,8},{8,9},{9,10},{10,1... | collective-permute-start | bytes 393224 | tf_op jit(solution)/shard_map/while/body/eval_jaxpr/ppermute | solution.py:15
  689.2 13.1 %collective-permute-start = (f32[16,8,256]{2,1,0:T(8,128)S(1)}, f32[16,8,256]{2,1,0:T(8,128)S(1)}, u32[]{:S(2)}, u32[]{:S(2)}) collective-permute-start(f32[16,8,256]{2,1,0:T(8,128)S(1)} %get-tuple-element.243), channel_id=1, source_target_pairs={{0,1},{1,2},{2,3},{3,4},{4,5},{5,6},{6,7},{7,8},{8,9},{9,10},{10,1... | collective-permute-start | bytes 393224 | tf_op jit(solution)/shard_map/while/body/eval_jaxpr/ppermute | solution.py:15
  702.3 12.5 %collective-permute-start = (f32[16,8,256]{2,1,0:T(8,128)S(1)}, f32[16,8,256]{2,1,0:T(8,128)S(1)}, u32[]{:S(2)}, u32[]{:S(2)}) collective-permute-start(f32[16,8,256]{2,1,0:T(8,128)S(1)} %get-tuple-element.243), channel_id=1, source_target_pairs={{0,1},{1,2},{2,3},{3,4},{4,5},{5,6},{6,7},{7,8},{8,9},{9,10},{10,1... | collective-permute-start | bytes 393224 | tf_op jit(solution)/shard_map/while/body/eval_jaxpr/ppermute | solution.py:15
  714.8 15.5 %collective-permute-start = (f32[16,8,256]{2,1,0:T(8,128)S(1)}, f32[16,8,256]{2,1,0:T(8,128)S(1)}, u32[]{:S(2)}, u32[]{:S(2)}) collective-permute-start(f32[16,8,256]{2,1,0:T(8,128)S(1)} %get-tuple-element.243), channel_id=1, source_target_pairs={{0,1},{1,2},{2,3},{3,4},{4,5},{5,6},{6,7},{7,8},{8,9},{9,10},{10,1... | collective-permute-start | bytes 393224 | tf_op jit(solution)/shard_map/while/body/eval_jaxpr/ppermute | solution.py:15
  730.4 12.5 %collective-permute-start = (f32[16,8,256]{2,1,0:T(8,128)S(1)}, f32[16,8,256]{2,1,0:T(8,128)S(1)}, u32[]{:S(2)}, u32[]{:S(2)}) collective-permute-start(f32[16,8,256]{2,1,0:T(8,128)S(1)} %get-tuple-element.243), channel_id=1, source_target_pairs={{0,1},{1,2},{2,3},{3,4},{4,5},{5,6},{6,7},{7,8},{8,9},{9,10},{10,1... | collective-permute-start | bytes 393224 | tf_op jit(solution)/shard_map/while/body/eval_jaxpr/ppermute | solution.py:15
  742.9 13.1 %collective-permute-start = (f32[16,8,256]{2,1,0:T(8,128)S(1)}, f32[16,8,256]{2,1,0:T(8,128)S(1)}, u32[]{:S(2)}, u32[]{:S(2)}) collective-permute-start(f32[16,8,256]{2,1,0:T(8,128)S(1)} %get-tuple-element.243), channel_id=1, source_target_pairs={{0,1},{1,2},{2,3},{3,4},{4,5},{5,6},{6,7},{7,8},{8,9},{9,10},{10,1... | collective-permute-start | bytes 393224 | tf_op jit(solution)/shard_map/while/body/eval_jaxpr/ppermute | solution.py:15
  756.1 12.5 %collective-permute-start = (f32[16,8,256]{2,1,0:T(8,128)S(1)}, f32[16,8,256]{2,1,0:T(8,128)S(1)}, u32[]{:S(2)}, u32[]{:S(2)}) collective-permute-start(f32[16,8,256]{2,1,0:T(8,128)S(1)} %get-tuple-element.243), channel_id=1, source_target_pairs={{0,1},{1,2},{2,3},{3,4},{4,5},{5,6},{6,7},{7,8},{8,9},{9,10},{10,1... | collective-permute-start | bytes 393224 | tf_op jit(solution)/shard_map/while/body/eval_jaxpr/ppermute | solution.py:15
  768.6 15.5 %collective-permute-start = (f32[16,8,256]{2,1,0:T(8,128)S(1)}, f32[16,8,256]{2,1,0:T(8,128)S(1)}, u32[]{:S(2)}, u32[]{:S(2)}) collective-permute-start(f32[16,8,256]{2,1,0:T(8,128)S(1)} %get-tuple-element.243), channel_id=1, source_target_pairs={{0,1},{1,2},{2,3},{3,4},{4,5},{5,6},{6,7},{7,8},{8,9},{9,10},{10,1... | collective-permute-start | bytes 393224 | tf_op jit(solution)/shard_map/while/body/eval_jaxpr/ppermute | solution.py:15
  784.1 12.5 %collective-permute-start = (f32[16,8,256]{2,1,0:T(8,128)S(1)}, f32[16,8,256]{2,1,0:T(8,128)S(1)}, u32[]{:S(2)}, u32[]{:S(2)}) collective-permute-start(f32[16,8,256]{2,1,0:T(8,128)S(1)} %get-tuple-element.243), channel_id=1, source_target_pairs={{0,1},{1,2},{2,3},{3,4},{4,5},{5,6},{6,7},{7,8},{8,9},{9,10},{10,1... | collective-permute-start | bytes 393224 | tf_op jit(solution)/shard_map/while/body/eval_jaxpr/ppermute | solution.py:15
  796.7 12.5 %collective-permute-start = (f32[16,8,256]{2,1,0:T(8,128)S(1)}, f32[16,8,256]{2,1,0:T(8,128)S(1)}, u32[]{:S(2)}, u32[]{:S(2)}) collective-permute-start(f32[16,8,256]{2,1,0:T(8,128)S(1)} %get-tuple-element.243), channel_id=1, source_target_pairs={{0,1},{1,2},{2,3},{3,4},{4,5},{5,6},{6,7},{7,8},{8,9},{9,10},{10,1... | collective-permute-start | bytes 393224 | tf_op jit(solution)/shard_map/while/body/eval_jaxpr/ppermute | solution.py:15
  809.2 0.7 copy-start.1
Sparse Core Ops, SparseCore 0:
  16.2 355.8 all-gather.1
where the time goes:
time: 830 us; the launch traced here: 817 us
  waiting for transfers between devices  349 us (42%)
  matrix products  192 us (23%)
  local copies, waits for them, and re-layouts  158 us (19%)
  starting transfers between devices  98.3 us (12%)
  between operations  13.5 us (2%)
    all_gather x1, waiting for transfers between devices, per_device(): panels = lax.all_gather(own_panels, 'src', axis=1, tiled=True)  349 us
    ppermute x31, starting transfers between devices, from_behind(): return lax.ppermute(value, axis, pairs)  98.3 us
    dot_general x32, matrix products, spectral_product(): jnp.einsum(layout_kind, left_im, right_im, preferred_element_type=jnp.flo...  45.8 us
    dot_general x32, matrix products, spectral_product(): jnp.einsum(layout_kind, left_im, right_re, preferred_element_type=jnp.flo...  45.7 us
    dot_general x32, matrix products, spectral_product(): jnp.einsum(layout_kind, left_re, right_im, preferred_element_type=jnp.flo...  45.7 us
    dot_general x32, matrix products, spectral_product(): jnp.einsum(layout_kind, left_re, right_re, preferred_element_type=jnp.flo...  45.5 us
    dot_general x32, local copies, waits for them, and re-layouts, spectral_product(): jnp.einsum(layout_kind, left_re, right_im, preferred_element_type=jnp.flo...  34.7 us
    dot_general x32, local copies, waits for them, and re-layouts, spectral_product(): jnp.einsum(layout_kind, left_im, right_re, preferred_element_type=jnp.flo...  34.7 us
  transfers between devices with their start and end apart: 32, of which 1 were waited for; matrix products, arithmetic and copies ran while one was open for 41% of the time, Pallas kernels for 0%

commit v1 on v0

v1 whole, which is shorter than its diff:
```python
import math

import jax
import jax.numpy as jnp
from jax import lax
from jax.sharding import PartitionSpec as P

F = 128
FBASE = 4
Y = 8
Q = 4


def fourier_table(samples):
    times = jnp.arange(samples, dtype=jnp.int32)
    freq_bins = FBASE + jnp.arange(F, dtype=jnp.int32)
    phases = times[:, None] * freq_bins[None, :] % samples
    angles = phases.astype(jnp.float32) * jnp.float32(2.0 * math.pi / samples)
    basis = jnp.concatenate([jnp.cos(angles), -jnp.sin(angles)], axis=1)
    return basis / jnp.float32(math.sqrt(samples))


def spectra(traces):
    samples = traces.shape[-1]
    rows = traces.reshape(-1, samples)
    out = lax.dot_general(
        fourier_table(samples), rows, (((0,), (1,)), ((), ())),
        precision=lax.Precision.HIGHEST, preferred_element_type=jnp.float32)
    return out.astype(jnp.bfloat16)


def per_device(src_traces, rec_traces):
    ns = lax.axis_size("src")
    ygroups = [[y * Q + q for y in range(Y)] for q in range(Q)]
    qgroups = [[y * Q + q for q in range(Q)] for y in range(Y)]
    s, x = src_traces.shape[:2]
    r = rec_traces.shape[1]
    weight = jnp.float32(1.0 / math.sqrt(x * Y * Q))

    def spread(traces):
        spec = spectra(traces)
        spec = spec.reshape(2, ns, Y, -1).transpose(1, 2, 0, 3)
        spec = lax.all_to_all(spec, "src", 0, 0)
        return lax.all_to_all(spec, "xl", 1, 0, axis_index_groups=ygroups)

    b = spread(rec_traces).reshape(Y, ns, 2, x, r)
    a = spread(src_traces).reshape(Y, ns, 2, s, x)
    b = b.transpose(2, 0, 3, 1, 4).reshape(2, Y * x, ns * r)
    a = a.transpose(2, 1, 3, 0, 4).reshape(2, ns * s, Y * x)

    def dot(u, v):
        return jnp.dot(u, v, preferred_element_type=jnp.float32)

    re = dot(a[0], b[0]) - dot(a[1], b[1])
    im = dot(a[0], b[1]) + dot(a[1], b[0])
    c = jnp.stack([re, im]) * weight
    c = c.reshape(2, ns, s, Y, Q, -1).transpose(4, 3, 1, 0, 2, 5)
    c = lax.psum_scatter(c, "xl", scatter_dimension=0, axis_index_groups=qgroups)
    c = lax.all_to_all(c, "xl", 0, 0, axis_index_groups=ygroups)
    c = lax.all_to_all(c, "src", 1, 0)
    c = c.transpose(3, 4, 2, 0, 1)
    return c.reshape(s, -1, 2 * F)


def solution(mesh):
    return jax.shard_map(
        per_device,
        mesh=mesh,
        in_specs=(P("src", "xl", None), P("xl", "src", None)),
        out_specs=P("src", "xl", None),
        check_vma=False,
    )
```

time: 830 us -> 247 us (0.30); the launches traced: 817 us -> 245 us
  waiting for transfers between devices: 349 us -> 125 us
  matrix products: 192 us -> 9.67 us
  local copies, waits for them, and re-layouts: 158 us -> 31.7 us
  starting transfers between devices: 98.3 us -> 25.9 us
  blocking collectives: 0 us -> 29.9 us
    all_gather x1 -> x0, waiting for transfers between devices: 349 us -> none  [per_device(): panels = lax.all_gather(own_panels, 'src', axis=1, tiled=True)]
    dot_general x130 -> x6, matrix products: 192 us -> 9.67 us  [the longest x2 8.8 us: spectra(): lax.dot_general(fourier_table(samples), rows, (((0,), (1,)), ((), ())), p...]
    dot_general x128 -> x0, local copies, waits for them, and re-layouts: 139 us -> none  [the longest x32 34.7 us: spectral_product(): jnp.einsum(layout_kind, left_re, right_im, preferred_element_type=jnp.flo...]
    unnamed x1 -> x2, waiting for transfers between devices: 0.02 us -> 103 us
    ppermute x31 -> x0, starting transfers between devices: 98.3 us -> none  [from_behind(): return lax.ppermute(value, axis, pairs)]
    all_to_all x0 -> x2, blocking collectives: none -> 29.9 us  [the longest x1 15.5 us: per_device(): c = lax.all_to_all(c, 'src', 1, 0)]
    all_to_all x0 -> x4, starting transfers between devices: none -> 25.7 us  [the longest x2 15.4 us: spread(): spec = lax.all_to_all(spec, 'src', 0, 0)]
    all_to_all x0 -> x4, waiting for transfers between devices: none -> 22.2 us  [the longest x2 13 us: spread(): spec = lax.all_to_all(spec, 'src', 0, 0)]
  transfers between devices with their start and end apart: 32 -> 5, of which waited for: 1 -> 5; matrix products, arithmetic and copies ran while one was open for 41% -> 7% of each run, Pallas kernels for 0% -> 0%
where the time goes in v1:
time: 247 us; the launch traced here: 245 us
  waiting for transfers between devices  125 us (51%)
  local copies, waits for them, and re-layouts  31.7 us (13%)
  blocking collectives  29.9 us (12%)
  starting transfers between devices  25.9 us (10%)
  between operations  13.6 us (6%)
  matrix products  9.67 us (4%)
  other arithmetic  8.97 us (4%)
    unnamed x2, waiting for transfers between devices  103 us
    all_to_all x1, blocking collectives, per_device(): c = lax.all_to_all(c, 'src', 1, 0)  15.5 us
    all_to_all x2, starting transfers between devices, spread(): spec = lax.all_to_all(spec, 'src', 0, 0)  15.4 us
    all_to_all x1, blocking collectives, per_device(): c = lax.all_to_all(c, 'xl', 0, 0, axis_index_groups=ygroups)  14.4 us
    all_to_all x2, waiting for transfers between devices, spread(): spec = lax.all_to_all(spec, 'src', 0, 0)  13 us
    all_to_all x2, starting transfers between devices, spread(): return lax.all_to_all(spec, 'xl', 1, 0, axis_index_groups=ygroups)  10.2 us
    all_to_all x2, waiting for transfers between devices, spread(): return lax.all_to_all(spec, 'xl', 1, 0, axis_index_groups=ygroups)  9.18 us
    slice x6, local copies, waits for them, and re-layouts, per_device(): re = dot(a[0], b[0]) - dot(a[1], b[1])  8.87 us
  transfers between devices with their start and end apart: 5, of which 5 were waited for; matrix products, arithmetic and copies ran while one was open for 7% of the time, Pallas kernels for 0%

profile of v1, /device:TPU:1, one launch (start us, length us, event | category | flops | bytes accessed | tf_op | source)
XLA Modules:
  0.0 244.8 jit_solution(14596027445234016915)
XLA Ops:
  6.5 0.0 copy-start
  6.5 2.1 fusion.9
  8.6 0.0 copy-done
  8.6 3.6 %convolution_convert_fusion = bf16[256,512]{1,0:T(8,128)(2,1)S(1)} fusion(f32[512,1024]{1,0:T(8,128)S(1)} %bitcast.86, f32[1024,128]{1,0:T(8,128)S(1)} %get-tuple-element.10, f32[1024,128]{1,0:T(8,128)S(1)} %get-tuple-element.9), kind=kOutput, calls=%fused_computation.2 | convolution fusion | flops 1611268096 | bytes 3407872 | tf_op jit(solution)/shard_map/dot_general | solution.py:26
  12.2 1.0 copy.41
  13.2 11.9 %all-to-all-start.2 = ((bf16[16,8,2,512]{3,2,1,0:T(2,128)(2,1)}), bf16[16,8,2,512]{3,2,1,0:T(2,128)(2,1)S(1)}, u32[]{:S(2)}, u32[]{:S(2)}) async-start(bf16[16,8,2,512]{3,2,1,0:T(2,128)(2,1)} %bitcast.96), calls=%async_computation.2 | async-start | bytes 524288 | tf_op jit(solution)/shard_map/all_to_all | solution.py:43
  25.1 5.2 %convolution_convert_fusion.1 = bf16[256,512]{1,0:T(8,128)(2,1)S(1)} fusion(f32[512,1024]{1,0:T(8,128)} %bitcast.91, f32[1024,128]{1,0:T(8,128)S(1)} %get-tuple-element.10, f32[1024,128]{1,0:T(8,128)S(1)} %get-tuple-element.9), kind=kOutput, calls=%fused_computation.3 | convolution fusion | flops 1611268096 | bytes 3407872 | tf_op jit(solution)/shard_map/dot_general | solution.py:26
  30.3 1.0 copy.42
  31.3 4.3 %all-to-all-done.2 = bf16[16,8,2,512]{3,2,1,0:T(2,128)(2,1)S(1)} async-done(((bf16[16,8,2,512]{3,2,1,0:T(2,128)(2,1)}), bf16[16,8,2,512]{3,2,1,0:T(2,128)(2,1)S(1)}, u32[]{:S(2)}, u32[]{:S(2)}) %all-to-all-start.2) | async-done | bytes 262176 | tf_op jit(solution)/shard_map/all_to_all | solution.py:43
  35.6 3.5 %all-to-all-start = ((bf16[16,8,2,512]{3,2,1,0:T(2,128)(2,1)}), bf16[16,8,2,512]{3,2,1,0:T(2,128)(2,1)S(1)}, u32[]{:S(2)}, u32[]{:S(2)}) async-start(bf16[16,8,2,512]{3,2,1,0:T(2,128)(2,1)} %bitcast.84), calls=%async_computation | async-start | bytes 524288 | tf_op jit(solution)/shard_map/all_to_all | solution.py:43
  39.1 0.8 copy.25
  40.0 8.7 %all-to-all-done = bf16[16,8,2,512]{3,2,1,0:T(2,128)(2,1)S(1)} async-done(((bf16[16,8,2,512]{3,2,1,0:T(2,128)(2,1)}), bf16[16,8,2,512]{3,2,1,0:T(2,128)(2,1)S(1)}, u32[]{:S(2)}, u32[]{:S(2)}) %all-to-all-start) | async-done | bytes 262176 | tf_op jit(solution)/shard_map/all_to_all | solution.py:43
  48.7 6.8 %all-to-all-start.3 = ((bf16[1,16,8,2,512]{4,1,3,0,2:T(8,128)(2,1)}), bf16[1,16,8,2,512]{4,1,3,0,2:T(8,128)(2,1)S(1)}, u32[]{:S(2)}, u32[]{:S(2)}) async-start(bf16[1,16,8,2,512]{4,1,3,0,2:T(8,128)(2,1)} %copy.25), calls=%async_computation.3 | async-start | bytes 524288 | tf_op jit(solution)/shard_map/all_to_all | solution.py:44
  55.5 0.8 copy.22
  56.4 8.5 %all-to-all-done.3 = bf16[1,16,8,2,512]{4,1,3,0,2:T(8,128)(2,1)S(1)} async-done(((bf16[1,16,8,2,512]{4,1,3,0,2:T(8,128)(2,1)}), bf16[1,16,8,2,512]{4,1,3,0,2:T(8,128)(2,1)S(1)}, u32[]{:S(2)}, u32[]{:S(2)}) %all-to-all-start.3) | async-done | bytes 262176 | tf_op jit(solution)/shard_map/all_to_all | solution.py:44
  64.9 3.4 %all-to-all-start.1 = ((bf16[1,16,8,2,512]{4,1,3,0,2:T(8,128)(2,1)}), bf16[1,16,8,2,512]{4,1,3,0,2:T(8,128)(2,1)S(1)}, u32[]{:S(2)}, u32[]{:S(2)}) async-start(bf16[1,16,8,2,512]{4,1,3,0,2:T(8,128)(2,1)} %copy.22), calls=%async_computation.1 | async-start | bytes 524288 | tf_op jit(solution)/shard_map/all_to_all | solution.py:44
  68.3 0.2 all-reduce.3.cloned.1.call-start
  68.5 2.7 %reshape_squeeze.7 = bf16[8,16,2,32,16]{4,3,1,2,0:T(8,128)(2,1)} reshape(bf16[8,1,16,1,2,512]{5,2,4,0,3,1:T(8,128)(2,1)S(1)} %bitcast.93) | data formatting | bytes 524288 | tf_op jit(solution)/shard_map/reshape;squeeze | solution.py:46
  71.2 3.0 %fusion.14 = (bf16[1,8,32,16,16]{4,2,3,0,1:T(8,128)(2,1)S(1)}, bf16[1,8,32,16,16]{4,2,3,0,1:T(8,128)(2,1)}) fusion(bf16[2,8,32,16,16]{4,2,3,0,1:T(8,128)(2,1)} %bitcast.87), kind=kLoop, calls=%fused_computation.28 | loop fusion | bytes 524288 | tf_op jit(solution)/shard_map/slice | solution.py:54
  74.2 1.2 copy.26
  75.4 1.4 squeeze.20
  76.8 0.7 all-to-all-done.1
  77.5 0.6 reshape_squeeze.6
  78.1 1.0 fusion.15
  79.1 0.0 copy-start.1
  79.1 1.1 copy.23
  80.3 1.4 squeeze.19
  81.7 0.0 copy-done.1
  81.7 1.2 copy.28
  82.9 1.4 squeeze.22
  84.4 1.4 copy.27
  85.7 0.4 squeeze.21
  86.1 0.2 fusion.16
  86.3 0.2 fusion.17
  86.5 0.2 convolution_subtract_fusion
  86.8 0.1 copy.29
  86.9 2.0 stack.9
  88.9 0.2 convolution_add_fusion
  89.2 0.1 copy.30
  89.3 2.0 stack.10
  91.3 5.0 %fusion = f32[4,8,16,2,16,8]{4,2,5,0,1,3:T(8,128)} fusion(f32[1,16,16,8,4,8]{2,1,5,4,3,0:T(8,128)} %stack.10, f32[1,16,16,8,4,8]{2,1,5,4,3,0:T(8,128)} %stack.9), kind=kLoop, calls=%fused_computation.1 | loop fusion | flops 262144 | bytes 1048576 | tf_op jit(solution)/shard_map/transpose | solution.py:57
  96.3 0.0 all-reduce.3.cloned.1.call-update
  96.3 1.3 dynamic-slice
  97.6 102.8 %all-reduce.3.cloned.1.call-done = f32[4,8,16,2,16,8]{4,2,5,0,1,3:T(8,128)} async-done(((f32[4,8,16,2,16,8]{4,2,5,0,1,3:T(8,128)}), f32[4,8,16,2,16,8]{4,2,5,0,1,3:T(8,128)}) %all-reduce.3.cloned.1.call-update) | async-done | bytes 524304
  200.4 2.0 copy_bitcast_fusion.3
  202.4 0.4 reshape.45
  202.8 14.4 %all_to_all.60 = f32[8,1,4096]{2,1,0:T(1,128)S(1)} all-to-all(f32[8,1,4096]{2,1,0:T(1,128)S(1)} %reshape.45), channel_id=1, replica_groups={{0,4,8,12,16,20,24,28},{1,5,9,13,17,21,25,29},{2,6,10,14,18,22,26,30},{..., dimensions={0} | all-to-all | bytes 262144 | tf_op jit(solution)/shard_map/all_to_all | solution.py:59
  217.2 0.5 broadcast.45
  217.7 1.0 reduce
  218.6 0.4 reshape.46
  219.0 0.1 bitcast_bitcast_fusion.1
  219.1 0.3 copy.43
  219.4 0.4 reshape.47
  219.8 15.5 %all_to_all.61 = f32[16,1,2048]{2,1,0:T(1,128)S(1)} all-to-all(f32[16,1,2048]{2,1,0:T(1,128)S(1)} %reshape.47), channel_id=1, replica_groups=mesh['src'=16,'xl'=32] {'src'}, dimensions={0} | all-to-all | bytes 262144 | tf_op jit(solution)/shard_map/all_to_all | solution.py:60
  235.3 0.9 reduce.1
  236.3 0.4 reshape.48
  236.7 0.1 bitcast_bitcast_fusion
  236.7 0.2 copy.33
  236.9 1.0 copy.34
  (1 shorter events, 0.0 us)
Async XLA Ops:
  6.5 2.1 copy-start
  13.2 22.4 %all-to-all-start.2 = ((bf16[16,8,2,512]{3,2,1,0:T(2,128)(2,1)}), bf16[16,8,2,512]{3,2,1,0:T(2,128)(2,1)S(1)}, u32[]{:S(2)}, u32[]{:S(2)}) async-start(bf16[16,8,2,512]{3,2,1,0:T(2,128)(2,1)} %bitcast.96), calls=%async_computation.2 | async-start | bytes 524288 | tf_op jit(solution)/shard_map/all_to_all | solution.py:43
  35.6 13.1 %all-to-all-start = ((bf16[16,8,2,512]{3,2,1,0:T(2,128)(2,1)}), bf16[16,8,2,512]{3,2,1,0:T(2,128)(2,1)S(1)}, u32[]{:S(2)}, u32[]{:S(2)}) async-start(bf16[16,8,2,512]{3,2,1,0:T(2,128)(2,1)} %bitcast.84), calls=%async_computation | async-start | bytes 524288 | tf_op jit(solution)/shard_map/all_to_all | solution.py:43
  48.7 16.2 %all-to-all-start.3 = ((bf16[1,16,8,2,512]{4,1,3,0,2:T(8,128)(2,1)}), bf16[1,16,8,2,512]{4,1,3,0,2:T(8,128)(2,1)S(1)}, u32[]{:S(2)}, u32[]{:S(2)}) async-start(bf16[1,16,8,2,512]{4,1,3,0,2:T(8,128)(2,1)} %copy.25), calls=%async_computation.3 | async-start | bytes 524288 | tf_op jit(solution)/shard_map/all_to_all | solution.py:44
  64.9 12.7 %all-to-all-start.1 = ((bf16[1,16,8,2,512]{4,1,3,0,2:T(8,128)(2,1)}), bf16[1,16,8,2,512]{4,1,3,0,2:T(8,128)(2,1)S(1)}, u32[]{:S(2)}, u32[]{:S(2)}) async-start(bf16[1,16,8,2,512]{4,1,3,0,2:T(8,128)(2,1)} %copy.22), calls=%async_computation.1 | async-start | bytes 524288 | tf_op jit(solution)/shard_map/all_to_all | solution.py:44
  68.3 132.1 %all-reduce.3.cloned.1.call-start = ((), (), s32[]{:S(2)}) async-start(), calls=%async_computation.6 | async-start | bytes 8388608
  79.1 2.6 %copy-start.1 = (bf16[1,8,32,16,16]{4,2,3,0,1:T(8,128)(2,1)S(1)}, bf16[1,8,32,16,16]{4,2,3,0,1:T(8,128)(2,1)}, u32[]{:S(2)}) copy-start(bf16[1,8,32,16,16]{4,2,3,0,1:T(8,128)(2,1)} %get-tuple-element.6) | copy-start | bytes 393220
Sparse Core Ops, SparseCore 0:
  96.4 103.9 all-reduce.2

commit v2 on v1

v2 whole, which is shorter than its diff:
```python
import functools
import math

import jax
import jax.numpy as jnp
import numpy as np
from jax import lax
from jax.experimental import pallas as pl
from jax.experimental.pallas import tpu as pltpu
from jax.sharding import PartitionSpec as P

F = 128
FBASE = 4
Q = 4
BF = jnp.bfloat16
F32 = jnp.float32
MESH = pl.DeviceIdType.MESH
NT = (((1,), (1,)), ((), ()))


def fourier_parts(samples):
    times = np.arange(samples, dtype=np.int64)
    bins = FBASE + np.arange(F, dtype=np.int64)
    angles = (bins[:, None] * times[None, :] % samples) * (2.0 * math.pi / samples)
    table = np.concatenate([np.cos(angles), -np.sin(angles)], axis=0) / math.sqrt(samples)
    table = table.astype(np.float32)
    high = table.astype(jnp.bfloat16)
    low = (table - high.astype(np.float32)).astype(jnp.bfloat16)
    return high, low


def dot_nt(a, b):
    return lax.dot_general(a, b, NT, preferred_element_type=F32)


def lane_bit(shape, bit):
    lanes = lax.broadcasted_iota(jnp.int32, shape, len(shape) - 1)
    return ((lanes >> bit) & 1) == 0


def kernel(ns, ny, scale, src_ref, rec_ref, thi_ref, tlo_ref, out_ref,
           xa, xb, th, tl, xh, xlo, u, s_buf, r1, r2, acat, bb,
           psend, precv, cown, xsend, xrecv, ck, d_buf, e_buf, t_buf, h_buf, g_buf,
           in_sem, s1_send, s1_recv, s2_send, s2_recv, loc_sem, p_sem, x_sem,
           c1_send, c1_recv, c2_send, c2_recv):
    me = lax.axis_index("src")
    j = lax.axis_index("xl")
    my_y = j // Q
    q = j % Q
    m = j // 2
    c = j % 2
    hi = m % 2
    nm = 2 * ny

    def load(a, b, k):
        return pltpu.make_async_copy(a, b, in_sem.at[k])

    loads = [load(thi_ref, th, 0), load(tlo_ref, tl, 1), load(src_ref, xa, 2)]
    rec_loads = [load(rec_ref.at[:, pl.ds(t * 128, 128)], xb.at[t], 3 + t) for t in range(8)]
    for item in loads + rec_loads:
        item.start()

    barrier = pltpu.get_barrier_semaphore()

    def greet_src(k, carry):
        pl.semaphore_signal(barrier, inc=1, device_id={"src": (me + k) % ns, "xl": j}, device_id_type=MESH)
        return carry

    def greet_m(k, carry):
        pl.semaphore_signal(barrier, inc=1, device_id={"src": me, "xl": ((m + k) % nm) * 2 + c}, device_id_type=MESH)
        return carry

    lax.fori_loop(1, ns, greet_src, 0)
    lax.fori_loop(1, nm, greet_m, 0)
    pl.semaphore_signal(barrier, inc=1, device_id={"src": me, "xl": m * 2 + 1 - c}, device_id_type=MESH)

    for item in loads:
        item.wait()

    def split(rows, start):
        high = rows.astype(BF)
        xh[pl.ds(start, rows.shape[0]), :] = high
        xlo[pl.ds(start, rows.shape[0]), :] = (rows - high.astype(F32)).astype(BF)

    def split_a(k, carry):
        at = pl.multiple_of(k * 64, 64)
        split(xa[pl.ds(at, 64), :], at)
        return carry

    def split_b(r, carry):
        slot = (r % 8) // 2 * 4 + (r // 8) * 2 + r % 2
        rows = jnp.concatenate([xb[t, pl.ds(r, 32, stride=16), :] for t in range(8)], axis=1)
        split(rows, pl.multiple_of(512 + slot * 32, 32))
        return carry

    def transform(n, carry):
        at = pl.multiple_of(n * 256, 256)
        high = xh[pl.ds(at, 256), :]
        low = xlo[pl.ds(at, 256), :]
        spec = dot_nt(th[...], high) + dot_nt(th[...], low) + dot_nt(tl[...], high)
        mask = lane_bit((F, 128), 5)
        for t in range(2):
            re = spec[:F, t * 128:(t + 1) * 128]
            im = spec[F:, t * 128:(t + 1) * 128]
            row = (n // 2) * 8 + (n % 2) * 4 + 2 * t
            u[pl.ds(row, F, stride=16), :] = jnp.where(mask, re, pltpu.roll(im, 32, 1))
            u[pl.ds(row + 1, F, stride=16), :] = jnp.where(mask, pltpu.roll(re, 96, 1), im)
        return carry

    lax.fori_loop(0, 8, split_a, 0)
    lax.fori_loop(0, 2, transform, 0)
    for item in rec_loads:
        item.wait()
    lax.fori_loop(0, 16, split_b, 0)
    lax.fori_loop(2, 4, transform, 0)

    pl.semaphore_wait(barrier, ns + nm - 1)

    def s1(k, to, frm):
        return pltpu.make_async_remote_copy(
            src_ref=s_buf.at[to], dst_ref=r1.at[frm], send_sem=s1_send.at[k], recv_sem=s1_recv.at[k],
            device_id={"src": to, "xl": j}, device_id_type=MESH)

    def s1_go(k, carry):
        to = (me + k) % ns
        s_buf[to] = u[pl.ds(pl.multiple_of(to * 128, 128), 128), :].astype(BF)
        s1(k, to, me).start()
        return carry

    lax.fori_loop(1, ns, s1_go, 0)
    r1[me] = u[pl.ds(pl.multiple_of(me * 128, 128), 128), :].astype(BF)

    def s1_wait(k, carry):
        s1(k, (me + k) % ns, (me + ns - k) % ns).wait()
        return carry

    lax.fori_loop(1, ns, s1_wait, 0)

    def s2(k, to, frm):
        return pltpu.make_async_remote_copy(
            src_ref=r1.at[:, pl.ds(pl.multiple_of(to * 16, 16), 16), :], dst_ref=r2.at[frm],
            send_sem=s2_send.at[k], recv_sem=s2_recv.at[k],
            device_id={"src": me, "xl": to * Q + q}, device_id_type=MESH)

    def s2_go(k, carry):
        s2(k, (my_y + k) % ny, my_y).start()
        return carry

    def s2_wait(k, carry):
        s2(k, (my_y + k) % ny, (my_y + ny - k) % ny).wait()
        return carry

    lax.fori_loop(1, ny, s2_go, 0)
    own = pltpu.make_async_copy(r1.at[:, pl.ds(pl.multiple_of(my_y * 16, 16), 16), :], r2.at[my_y], loc_sem)
    own.start()
    own.wait()
    lax.fori_loop(1, ny, s2_wait, 0)

    def arrange(i2, carry):
        top = lane_bit((16, 128), 6)
        real = lane_bit((16, 128), 5)
        for p in range(4):
            w = []
            for e in range(2):
                u0 = r2[2 * p, 2 * i2 + e].astype(F32)
                u1 = r2[2 * p + 1, 2 * i2 + e].astype(F32)
                w.append((jnp.where(top, u0, pltpu.roll(u1, 64, 1)), jnp.where(top, pltpu.roll(u0, 64, 1), u1)))
                rows = jnp.concatenate([w[e][0][:8], w[e][1][:8]], axis=0)
                acat[pl.ds(pl.multiple_of(i2 * 32 + e * 16, 16), 16), p * 128:(p + 1) * 128] = rows.astype(BF)
            for ra in range(2):
                rows = jnp.concatenate([w[0][ra][8:], w[1][ra][8:]], axis=0)
                at = pl.multiple_of(i2 * 16, 16)
                bb[ra, pl.ds(at, 16), p * 128:(p + 1) * 128] = jnp.where(real, rows, -rows).astype(BF)
                swapped = jnp.where(real, pltpu.roll(rows, 96, 1), pltpu.roll(rows, 32, 1))
                bb[ra, pl.ds(128 + at, 16), p * 128:(p + 1) * 128] = swapped.astype(BF)
        return carry

    lax.fori_loop(0, ns // 2, arrange, 0)

    prod = dot_nt(acat[...], bb[1 - c])
    psend[0] = prod[:, :128]
    psend[1] = prod[:, 128:]
    pair = pltpu.make_async_remote_copy(
        src_ref=psend, dst_ref=precv, send_sem=p_sem.at[0], recv_sem=p_sem.at[1],
        device_id={"src": me, "xl": m * 2 + 1 - c}, device_id_type=MESH)
    pair.start()
    prod = dot_nt(acat[...], bb[c])
    cown[0] = prod[:, :128]
    cown[1] = prod[:, 128:]
    pair.wait()

    theirs = pl.ds(pl.multiple_of((1 - hi) * 128, 128), 128)
    mine = pl.ds(pl.multiple_of(hi * 128, 128), 128)
    for z in range(2):
        xsend[z] = (cown[z, theirs, :] + precv[z, theirs, :]).astype(BF)
    cross = pltpu.make_async_remote_copy(
        src_ref=xsend, dst_ref=xrecv, send_sem=x_sem.at[0], recv_sem=x_sem.at[1],
        device_id={"src": me, "xl": (my_y * 2 + 1 - hi) * 2 + c}, device_id_type=MESH)
    cross.start()
    for z in range(2):
        ck[pl.ds(z * 128, 128), :] = cown[z, mine, :] + precv[z, mine, :]
    cross.wait()
    for z in range(2):
        ck[pl.ds(z * 128, 128), :] += xrecv[z].astype(F32)

    halves = []
    for z in range(2):
        v = jnp.concatenate([ck[pl.ds(z * 128 + sp, 8, stride=16), :] for sp in range(16)], axis=0)
        for b in range(4):
            step = 8 << b
            v = v.reshape(8 >> b, 2, 8 << b, 128)
            low, high = v[:, 0].reshape(64, 128), v[:, 1].reshape(64, 128)
            keep = lane_bit((64, 128), b + 3)
            new_low = jnp.where(keep, low, pltpu.roll(high, step, 1))
            new_high = jnp.where(keep, pltpu.roll(low, 128 - step, 1), high)
            parts = (8 >> b, 1, 8 << b, 128)
            v = jnp.concatenate([new_low.reshape(parts), new_high.reshape(parts)], axis=1).reshape(128, 128)
        halves.append(v.reshape(16, 8, 128))
    d_buf[...] = jnp.concatenate(halves, axis=1).astype(BF)

    def c1(k, to, frm):
        return pltpu.make_async_remote_copy(
            src_ref=d_buf.at[to], dst_ref=e_buf.at[frm], send_sem=c1_send.at[k], recv_sem=c1_recv.at[k],
            device_id={"src": me, "xl": to * 2 + c}, device_id_type=MESH)

    def c1_go(k, carry):
        c1(k, (m + k) % nm, m).start()
        return carry

    def c1_wait(k, carry):
        c1(k, (m + k) % nm, (m + nm - k) % nm).wait()
        return carry

    lax.fori_loop(1, nm, c1_go, 0)
    e_buf[m] = d_buf[m]
    lax.fori_loop(1, nm, c1_wait, 0)

    for half in range(2):
        for y in range(ny):
            tile = e_buf[2 * y + half].astype(F32)
            t_buf[pl.ds(half * 128 + y, 8, stride=16), :] = tile[:8]
            t_buf[pl.ds(half * 128 + 8 + y, 8, stride=16), :] = tile[8:]
    h_buf[...] = t_buf[...].reshape(16, 16, 128).astype(BF)

    def c2(k, to, frm):
        return pltpu.make_async_remote_copy(
            src_ref=h_buf.at[to], dst_ref=g_buf.at[frm], send_sem=c2_send.at[k], recv_sem=c2_recv.at[k],
            device_id={"src": to, "xl": j}, device_id_type=MESH)

    def c2_go(k, carry):
        c2(k, (me + k) % ns, me).start()
        return carry

    def c2_wait(k, carry):
        c2(k, (me + k) % ns, (me + ns - k) % ns).wait()
        return carry

    lax.fori_loop(1, ns, c2_go, 0)
    g_buf[me] = h_buf[me]
    lax.fori_loop(1, ns, c2_wait, 0)

    got = g_buf[...].astype(F32)
    for z in range(2):
        flat = got[:, z * 8:(z + 1) * 8, :].reshape(F, 128)
        turned = flat.T * scale
        for s in range(16):
            sp = (s >> 1 & 1) * 8 + (s >> 2) * 2 + (s & 1)
            out_ref[s, :, z * F:(z + 1) * F] = turned[sp * 8:(sp + 1) * 8]


def per_device(ns, nx, src_traces, rec_traces):
    ny = nx // Q
    s, x, samples = src_traces.shape
    r = rec_traces.shape[1]
    scale = 1.0 / math.sqrt(x * nx)
    high, low = fourier_parts(samples)
    rows = s * x
    rec = rec_traces.reshape(rows, samples)
    out_shape = jax.ShapeDtypeStruct((s, r * ns // nx, 2 * F), F32)
    dma = pltpu.SemaphoreType.DMA
    nm = 2 * ny
    any_spec = pl.BlockSpec(memory_space=pl.ANY)
    return pl.pallas_call(
        functools.partial(kernel, ns, ny, scale),
        out_shape=out_shape,
        in_specs=[any_spec] * 4,
        out_specs=pl.BlockSpec(memory_space=pltpu.VMEM),
        scratch_shapes=[
            pltpu.VMEM((rows, samples), F32),
            pltpu.VMEM((8, rows, 128), F32),
            pltpu.VMEM((2 * F, samples), BF),
            pltpu.VMEM((2 * F, samples), BF),
            pltpu.VMEM((2 * rows, samples), BF),
            pltpu.VMEM((2 * rows, samples), BF),
            pltpu.VMEM((F * 16, 128), F32),
            pltpu.VMEM((ns, 128, 128), BF),
            pltpu.VMEM((ns, 128, 128), BF),
            pltpu.VMEM((ny, ns, 16, 128), BF),
            pltpu.VMEM((256, 512), BF),
            pltpu.VMEM((2, 256, 512), BF),
            pltpu.VMEM((2, 256, 128), F32),
            pltpu.VMEM((2, 256, 128), F32),
            pltpu.VMEM((2, 256, 128), F32),
            pltpu.VMEM((2, 128, 128), BF),
            pltpu.VMEM((2, 128, 128), BF),
            pltpu.VMEM((256, 128), F32),
            pltpu.VMEM((16, 16, 128), BF),
            pltpu.VMEM((16, 16, 128), BF),
            pltpu.VMEM((256, 128), F32),
            pltpu.VMEM((16, 16, 128), BF),
            pltpu.VMEM((16, 16, 128), BF),
            dma((11,)), dma((ns,)), dma((ns,)), dma((ny,)), dma((ny,)), dma, dma((2,)), dma((2,)),
            dma((nm,)), dma((nm,)), dma((ns,)), dma((ns,)),
        ],
        compiler_params=pltpu.CompilerParams(
            collective_id=0, has_side_effects=True, vmem_limit_bytes=56 << 20),
    )(src_traces.reshape(rows, samples), rec, jnp.asarray(high), jnp.asarray(low))


def solution(mesh):
    body = functools.partial(per_device, mesh.shape["src"], mesh.shape["xl"])
    return jax.shard_map(
        body,
        mesh=mesh,
        in_specs=(P("src", "xl", None), P("xl", "src", None)),
        out_specs=P("src", "xl", None),
        check_vma=False,
    )
```

time: 247 us -> 64.4 us (0.26)
  waiting for transfers between devices: 125 us -> 0 us
  Pallas kernels: 0 us -> 62.4 us
  local copies, waits for them, and re-layouts: 31.7 us -> 1.57 us
  blocking collectives: 29.9 us -> 0 us
  starting transfers between devices: 25.9 us -> 0 us
  between operations: 13.6 us -> 0.01 us
  matrix products: 9.67 us -> 0 us
  other arithmetic: 8.97 us -> 0 us
    unnamed x2 -> x0, waiting for transfers between devices: 103 us -> none
    pallas_call x0 -> x1, Pallas kernels: none -> 62.4 us  [per_device(): pl.pallas_call(functools.partial(kernel, ns, ny, scale), out_shape=out_sh...]
    all_to_all x2 -> x0, blocking collectives: 29.9 us -> none  [the longest x1 15.5 us: per_device(): c = lax.all_to_all(c, 'src', 1, 0)]
    all_to_all x4 -> x0, starting transfers between devices: 25.7 us -> none  [the longest x2 15.4 us: spread(): spec = lax.all_to_all(spec, 'src', 0, 0)]
    all_to_all x4 -> x0, waiting for transfers between devices: 22.2 us -> none  [the longest x2 13 us: spread(): spec = lax.all_to_all(spec, 'src', 0, 0)]
    dot_general x6 -> x0, matrix products: 9.67 us -> none  [the longest x2 8.8 us: spectra(): lax.dot_general(fourier_table(samples), rows, (((0,), (1,)), ((), ())), p...]
    slice x6 -> x0, local copies, waits for them, and re-layouts: 8.87 us -> none  [per_device(): re = dot(a[0], b[0]) - dot(a[1], b[1])]
    another operation x4 -> x0, local copies, waits for them, and re-layouts: 7.31 us -> none  [the longest x2 4.01 us: per_device(): c = jnp.stack([re, im]) * weight]
  transfers between devices with their start and end apart: 5 -> 0, of which waited for: 5 -> 0; matrix products, arithmetic and copies ran while one was open for 7% -> 0% of each run, Pallas kernels for 0% -> 0%
where the time goes in v2:
time: 64.4 us; the launch traced here: 63.9 us
  Pallas kernels  62.4 us (97%)
  local copies, waits for them, and re-layouts  1.57 us (2%)
    pallas_call x1, Pallas kernels, per_device(): pl.pallas_call(functools.partial(kernel, ns, ny, scale), out_shape=out_sh...  62.4 us
    unnamed x1, local copies, waits for them, and re-layouts  1.57 us

profile of v2, /device:TPU:1, one launch (start us, length us, event | category | flops | bytes accessed | tf_op | source)
XLA Modules:
  0.0 63.9 jit_solution(13370680303304892781)
XLA Ops:
  0.0 62.4 %shard_map.46 = f32[16,8,256]{2,1,0:T(8,128)} custom-call(f32[512,1024]{1,0:T(8,128)} %bitcast.2, f32[512,1024]{1,0:T(8,128)} %bitcast.3, bf16[256,1024]{1,0:T(8,128)(2,1)} %constant.4.clone.thi_ref, bf16[256,1024]{1,0:T(8,128)(2,1)} %constant.5.clone.tlo_ref), custom_call_target="tpu_custom_call" | custom-call | tf_op jit(solution)/shard_map/pallas_call | solution.py:283
  62.4 1.6 %copy.6 = f32[16,8,256]{2,1,0:T(8,128)} copy(f32[16,8,256]{2,1,0:T(8,128)} %shard_map.46) | data formatting | bytes 262144

commit v3 on v2

--- a/solution.py
+++ b/solution.py
@@ -39,9 +39,9 @@
 
 
 def kernel(ns, ny, scale, src_ref, rec_ref, thi_ref, tlo_ref, out_ref,
-           xa, xb, th, tl, xh, xlo, u, s_buf, r1, r2, acat, bb,
+           xa, xb, th, tl, xh, xlo, u, s_buf, r2, acat, bb,
            psend, precv, cown, xsend, xrecv, ck, d_buf, e_buf, t_buf, h_buf, g_buf,
-           in_sem, s1_send, s1_recv, s2_send, s2_recv, loc_sem, p_sem, x_sem,
+           in_sem, s_send, s_recv, p_sem, x_sem,
            c1_send, c1_recv, c2_send, c2_recv):
     me = lax.axis_index("src")
     j = lax.axis_index("xl")
@@ -62,16 +62,17 @@
 
     barrier = pltpu.get_barrier_semaphore()
 
-    def greet_src(k, carry):
-        pl.semaphore_signal(barrier, inc=1, device_id={"src": (me + k) % ns, "xl": j}, device_id_type=MESH)
-        return carry
-
-    def greet_m(k, carry):
-        pl.semaphore_signal(barrier, inc=1, device_id={"src": me, "xl": ((m + k) % nm) * 2 + c}, device_id_type=MESH)
-        return carry
-
-    lax.fori_loop(1, ns, greet_src, 0)
-    lax.fori_loop(1, nm, greet_m, 0)
+    def greet(k, carry):
+        to = {"src": (me + k // ny) % ns, "xl": (my_y + k) % ny * Q + q}
+        pl.semaphore_signal(barrier, inc=1, device_id=to, device_id_type=MESH)
+        return carry
+
+    def greet_x(k, carry):
+        pl.semaphore_signal(barrier, inc=1, device_id={"src": me, "xl": k * Q + (1 - hi) * 2 + c}, device_id_type=MESH)
+        return carry
+
+    lax.fori_loop(1, ns * ny, greet, 0)
+    lax.fori_loop(0, ny, greet_x, 0)
     pl.semaphore_signal(barrier, inc=1, device_id={"src": me, "xl": m * 2 + 1 - c}, device_id_type=MESH)
 
     for item in loads:
@@ -114,56 +115,35 @@
     lax.fori_loop(0, 16, split_b, 0)
     lax.fori_loop(2, 4, transform, 0)
 
-    pl.semaphore_wait(barrier, ns + nm - 1)
-
-    def s1(k, to, frm):
-        return pltpu.make_async_remote_copy(
-            src_ref=s_buf.at[to], dst_ref=r1.at[frm], send_sem=s1_send.at[k], recv_sem=s1_recv.at[k],
-            device_id={"src": to, "xl": j}, device_id_type=MESH)
-
-    def s1_go(k, carry):
+    pl.semaphore_wait(barrier, ns * ny + ny)
+
+    def convert(k, carry):
         to = (me + k) % ns
-        s_buf[to] = u[pl.ds(pl.multiple_of(to * 128, 128), 128), :].astype(BF)
-        s1(k, to, me).start()
-        return carry
-
-    lax.fori_loop(1, ns, s1_go, 0)
-    r1[me] = u[pl.ds(pl.multiple_of(me * 128, 128), 128), :].astype(BF)
-
-    def s1_wait(k, carry):
-        s1(k, (me + k) % ns, (me + ns - k) % ns).wait()
-        return carry
-
-    lax.fori_loop(1, ns, s1_wait, 0)
-
-    def s2(k, to, frm):
-        return pltpu.make_async_remote_copy(
-            src_ref=r1.at[:, pl.ds(pl.multiple_of(to * 16, 16), 16), :], dst_ref=r2.at[frm],
-            send_sem=s2_send.at[k], recv_sem=s2_recv.at[k],
-            device_id={"src": me, "xl": to * Q + q}, device_id_type=MESH)
-
-    def s2_go(k, carry):
-        s2(k, (my_y + k) % ny, my_y).start()
-        return carry
-
-    def s2_wait(k, carry):
-        s2(k, (my_y + k) % ny, (my_y + ny - k) % ny).wait()
-        return carry
-
-    lax.fori_loop(1, ny, s2_go, 0)
-    own = pltpu.make_async_copy(r1.at[:, pl.ds(pl.multiple_of(my_y * 16, 16), 16), :], r2.at[my_y], loc_sem)
-    own.start()
-    own.wait()
-    lax.fori_loop(1, ny, s2_wait, 0)
+        s_buf[to] = u[pl.ds(pl.multiple_of(to * 128, 128), 128), :].astype(BF).reshape(8, 16, 128)
+
+        def go(y, inner):
+            to_y = (my_y + y) % ny
+            pltpu.make_async_remote_copy(
+                src_ref=s_buf.at[to, to_y], dst_ref=r2.at[me, my_y], send_sem=s_send, recv_sem=s_recv.at[me],
+                device_id={"src": to, "xl": to_y * Q + q}, device_id_type=MESH).start()
+            return inner
+
+        lax.fori_loop(lax.select(k == 0, 1, 0), ny, go, 0)
+        return carry
+
+    lax.fori_loop(0, ns, convert, 0)
+    pltpu.make_async_copy(s_buf.at[me, my_y], r2.at[me, my_y], s_recv.at[me]).start()
 
     def arrange(i2, carry):
         top = lane_bit((16, 128), 6)
         real = lane_bit((16, 128), 5)
+        for e in range(2):
+            pltpu.make_async_copy(r2.at[2 * i2 + e], r2.at[2 * i2 + e], s_recv.at[2 * i2 + e]).wait()
         for p in range(4):
             w = []
             for e in range(2):
-                u0 = r2[2 * p, 2 * i2 + e].astype(F32)
-                u1 = r2[2 * p + 1, 2 * i2 + e].astype(F32)
+                u0 = r2[2 * i2 + e, 2 * p].astype(F32)
+                u1 = r2[2 * i2 + e, 2 * p + 1].astype(F32)
                 w.append((jnp.where(top, u0, pltpu.roll(u1, 64, 1)), jnp.where(top, pltpu.roll(u0, 64, 1), u1)))
                 rows = jnp.concatenate([w[e][0][:8], w[e][1][:8]], axis=0)
                 acat[pl.ds(pl.multiple_of(i2 * 32 + e * 16, 16), 16), p * 128:(p + 1) * 128] = rows.astype(BF)
@@ -176,6 +156,8 @@
         return carry
 
     lax.fori_loop(0, ns // 2, arrange, 0)
+    for part in (s_buf.at[pl.ds(0, ns - 1)], s_buf.at[0, pl.ds(0, ny - 1)]):
+        pltpu.make_async_copy(part, part, s_send).wait()
 
     prod = dot_nt(acat[...], bb[1 - c])
     psend[0] = prod[:, :128]
@@ -293,9 +275,8 @@
             pltpu.VMEM((2 * rows, samples), BF),
             pltpu.VMEM((2 * rows, samples), BF),
             pltpu.VMEM((F * 16, 128), F32),
-            pltpu.VMEM((ns, 128, 128), BF),
-            pltpu.VMEM((ns, 128, 128), BF),
-            pltpu.VMEM((ny, ns, 16, 128), BF),
+            pltpu.VMEM((ns, ny, 16, 128), BF),
+            pltpu.VMEM((ns, ny, 16, 128), BF),
             pltpu.VMEM((256, 512), BF),
             pltpu.VMEM((2, 256, 512), BF),
             pltpu.VMEM((2, 256, 128), F32),
@@ -309,7 +290,7 @@
             pltpu.VMEM((256, 128), F32),
             pltpu.VMEM((16, 16, 128), BF),
             pltpu.VMEM((16, 16, 128), BF),
-            dma((11,)), dma((ns,)), dma((ns,)), dma((ny,)), dma((ny,)), dma, dma((2,)), dma((2,)),
+            dma((11,)), dma, dma((ns,)), dma((2,)), dma((2,)),
             dma((nm,)), dma((nm,)), dma((ns,)), dma((ns,)),
         ],
         compiler_params=pltpu.CompilerParams(

time: 64.4 us -> 57.7 us (0.90)
  the two profiles are of different devices: /device:TPU:1 before, /device:TPU:4 now
where the time goes in v3:
time: 57.7 us; the launch traced here: 57.6 us
  Pallas kernels  56 us (97%)
  local copies, waits for them, and re-layouts  1.57 us (3%)
    pallas_call x1, Pallas kernels, per_device(): pl.pallas_call(functools.partial(kernel, ns, ny, scale), out_shape=out_sh...  56 us
    unnamed x1, local copies, waits for them, and re-layouts  1.57 us

profile of v3, /device:TPU:4, one launch (start us, length us, event | category | flops | bytes accessed | tf_op | source)
XLA Modules:
  0.0 57.6 jit_solution(7452168469525627254)
XLA Ops:
  0.0 56.0 %shard_map.46 = f32[16,8,256]{2,1,0:T(8,128)} custom-call(f32[512,1024]{1,0:T(8,128)} %bitcast.2, f32[512,1024]{1,0:T(8,128)} %bitcast.3, bf16[256,1024]{1,0:T(8,128)(2,1)} %constant.4.clone.thi_ref, bf16[256,1024]{1,0:T(8,128)(2,1)} %constant.5.clone.tlo_ref), custom_call_target="tpu_custom_call" | custom-call | tf_op jit(solution)/shard_map/pallas_call | solution.py:265
  56.0 1.6 %copy.6 = f32[16,8,256]{2,1,0:T(8,128)} copy(f32[16,8,256]{2,1,0:T(8,128)} %shard_map.46) | data formatting | bytes 262144

commit v4 on v3

--- a/solution.py
+++ b/solution.py
@@ -42,7 +42,7 @@
            xa, xb, th, tl, xh, xlo, u, s_buf, r2, acat, bb,
            psend, precv, cown, xsend, xrecv, ck, d_buf, e_buf, t_buf, h_buf, g_buf,
            in_sem, s_send, s_recv, p_sem, x_sem,
-           c1_send, c1_recv, c2_send, c2_recv):
+           c1_send, c1_recv, c2_send, c2_recv, ready):
     me = lax.axis_index("src")
     j = lax.axis_index("xl")
     my_y = j // Q
@@ -62,16 +62,24 @@
 
     barrier = pltpu.get_barrier_semaphore()
 
-    def greet(k, carry):
-        to = {"src": (me + k // ny) % ns, "xl": (my_y + k) % ny * Q + q}
-        pl.semaphore_signal(barrier, inc=1, device_id=to, device_id_type=MESH)
+    def greet_src(k, carry):
+        pl.semaphore_signal(barrier, inc=1, device_id={"src": (me + k) % ns, "xl": j}, device_id_type=MESH)
+        return carry
+
+    def greet_y(k, carry):
+        pl.semaphore_signal(barrier, inc=1, device_id={"src": me, "xl": (my_y + k) % ny * Q + q}, device_id_type=MESH)
+        return carry
+
+    def row_ready(k, carry):
+        pl.semaphore_signal(ready, inc=1, device_id={"src": (me + k) % ns, "xl": j}, device_id_type=MESH)
         return carry
 
     def greet_x(k, carry):
         pl.semaphore_signal(barrier, inc=1, device_id={"src": me, "xl": k * Q + (1 - hi) * 2 + c}, device_id_type=MESH)
         return carry
 
-    lax.fori_loop(1, ns * ny, greet, 0)
+    lax.fori_loop(1, ns, greet_src, 0)
+    lax.fori_loop(1, ny, greet_y, 0)
     lax.fori_loop(0, ny, greet_x, 0)
     pl.semaphore_signal(barrier, inc=1, device_id={"src": me, "xl": m * 2 + 1 - c}, device_id_type=MESH)
 
@@ -115,23 +123,22 @@
     lax.fori_loop(0, 16, split_b, 0)
     lax.fori_loop(2, 4, transform, 0)
 
-    pl.semaphore_wait(barrier, ns * ny + ny)
-
-    def convert(k, carry):
-        to = (me + k) % ns
-        s_buf[to] = u[pl.ds(pl.multiple_of(to * 128, 128), 128), :].astype(BF).reshape(8, 16, 128)
-
-        def go(y, inner):
-            to_y = (my_y + y) % ny
-            pltpu.make_async_remote_copy(
-                src_ref=s_buf.at[to, to_y], dst_ref=r2.at[me, my_y], send_sem=s_send, recv_sem=s_recv.at[me],
-                device_id={"src": to, "xl": to_y * Q + q}, device_id_type=MESH).start()
-            return inner
-
-        lax.fori_loop(lax.select(k == 0, 1, 0), ny, go, 0)
-        return carry
-
-    lax.fori_loop(0, ns, convert, 0)
+    pl.semaphore_wait(barrier, ns + 2 * ny - 1)
+    lax.fori_loop(1, ns, row_ready, 0)
+    for k in range(ns):
+        s_buf[k] = u[k * 128:(k + 1) * 128, :].astype(BF).reshape(8, 16, 128)
+    pl.semaphore_wait(ready, ns - 1)
+
+    def go(k, carry):
+        order = k * 37 % (ns * ny)
+        to = (me + order // ny) % ns
+        to_y = (my_y + order) % ny
+        pltpu.make_async_remote_copy(
+            src_ref=s_buf.at[to, to_y], dst_ref=r2.at[me, my_y], send_sem=s_send, recv_sem=s_recv.at[me],
+            device_id={"src": to, "xl": to_y * Q + q}, device_id_type=MESH).start()
+        return carry
+
+    lax.fori_loop(1, ns * ny, go, 0)
     pltpu.make_async_copy(s_buf.at[me, my_y], r2.at[me, my_y], s_recv.at[me]).start()
 
     def arrange(i2, carry):
@@ -291,7 +298,7 @@
             pltpu.VMEM((16, 16, 128), BF),
             pltpu.VMEM((16, 16, 128), BF),
             dma((11,)), dma, dma((ns,)), dma((2,)), dma((2,)),
-            dma((nm,)), dma((nm,)), dma((ns,)), dma((ns,)),
+            dma((nm,)), dma((nm,)), dma((ns,)), dma((ns,)), pltpu.SemaphoreType.REGULAR,
         ],
         compiler_params=pltpu.CompilerParams(
             collective_id=0, has_side_effects=True, vmem_limit_bytes=56 << 20),

time: 57.7 us -> 56.9 us (0.986)
  the two profiles are of different devices: /device:TPU:4 before, /device:TPU:1 now
where the time goes in v4:
time: 56.9 us; the launch traced here: 56 us
  Pallas kernels  54.4 us (96%)
  local copies, waits for them, and re-layouts  1.57 us (3%)
    pallas_call x1, Pallas kernels, per_device(): pl.pallas_call(functools.partial(kernel, ns, ny, scale), out_shape=out_sh...  54.4 us
    unnamed x1, local copies, waits for them, and re-layouts  1.57 us

profile of v4, /device:TPU:1, one launch (start us, length us, event | category | flops | bytes accessed | tf_op | source)
XLA Modules:
  0.0 56.0 jit_solution(14131203829291750868)
XLA Ops:
  0.0 54.4 %shard_map.46 = f32[16,8,256]{2,1,0:T(8,128)} custom-call(f32[512,1024]{1,0:T(8,128)} %bitcast.2, f32[512,1024]{1,0:T(8,128)} %bitcast.3, bf16[256,1024]{1,0:T(8,128)(2,1)} %constant.4.clone.thi_ref, bf16[256,1024]{1,0:T(8,128)(2,1)} %constant.5.clone.tlo_ref), custom_call_target="tpu_custom_call" | custom-call | tf_op jit(solution)/shard_map/pallas_call | solution.py:272
  54.4 1.6 %copy.6 = f32[16,8,256]{2,1,0:T(8,128)} copy(f32[16,8,256]{2,1,0:T(8,128)} %shard_map.46) | data formatting | bytes 262144

commit v5 on v4

--- a/solution.py
+++ b/solution.py
@@ -40,8 +40,8 @@
 
 def kernel(ns, ny, scale, src_ref, rec_ref, thi_ref, tlo_ref, out_ref,
            xa, xb, th, tl, xh, xlo, u, s_buf, r2, acat, bb,
-           psend, precv, cown, xsend, xrecv, ck, d_buf, e_buf, t_buf, h_buf, g_buf,
-           in_sem, s_send, s_recv, p_sem, x_sem,
+           psend, precv, cown, ck, d_buf, e_buf, t_buf, h_buf, g_buf,
+           in_sem, s_send, s_recv, p_sem,
            c1_send, c1_recv, c2_send, c2_recv, ready):
     me = lax.axis_index("src")
     j = lax.axis_index("xl")
@@ -117,28 +117,39 @@
         return carry
 
     lax.fori_loop(0, 8, split_a, 0)
+    pl.semaphore_wait(barrier, ns + 2 * ny - 1)
+    lax.fori_loop(1, ns, row_ready, 0)
     lax.fori_loop(0, 2, transform, 0)
     for item in rec_loads:
         item.wait()
     lax.fori_loop(0, 16, split_b, 0)
     lax.fori_loop(2, 4, transform, 0)
 
-    pl.semaphore_wait(barrier, ns + 2 * ny - 1)
-    lax.fori_loop(1, ns, row_ready, 0)
     for k in range(ns):
         s_buf[k] = u[k * 128:(k + 1) * 128, :].astype(BF).reshape(8, 16, 128)
-    pl.semaphore_wait(ready, ns - 1)
-
-    def go(k, carry):
-        order = k * 37 % (ns * ny)
-        to = (me + order // ny) % ns
-        to_y = (my_y + order) % ny
+
+    def send(to, to_y):
         pltpu.make_async_remote_copy(
             src_ref=s_buf.at[to, to_y], dst_ref=r2.at[me, my_y], send_sem=s_send, recv_sem=s_recv.at[me],
             device_id={"src": to, "xl": to_y * Q + q}, device_id_type=MESH).start()
-        return carry
-
-    lax.fori_loop(1, ns * ny, go, 0)
+
+    def go_column(k, carry):
+        send((me + k) % ns, my_y)
+        return carry
+
+    def go_row(k, carry):
+        send(me, (my_y + k) % ny)
+        return carry
+
+    def go(k, carry):
+        order = k * 37 % ((ns - 1) * (ny - 1))
+        send((me + 1 + order // (ny - 1)) % ns, (my_y + 1 + order % (ny - 1)) % ny)
+        return carry
+
+    lax.fori_loop(1, ny, go_row, 0)
+    lax.fori_loop(1, ns, go_column, 0)
+    pl.semaphore_wait(ready, ns - 1)
+    lax.fori_loop(0, (ns - 1) * (ny - 1), go, 0)
     pltpu.make_async_copy(s_buf.at[me, my_y], r2.at[me, my_y], s_recv.at[me]).start()
 
     def arrange(i2, carry):
@@ -178,33 +189,22 @@
     cown[1] = prod[:, 128:]
     pair.wait()
 
-    theirs = pl.ds(pl.multiple_of((1 - hi) * 128, 128), 128)
-    mine = pl.ds(pl.multiple_of(hi * 128, 128), 128)
     for z in range(2):
-        xsend[z] = (cown[z, theirs, :] + precv[z, theirs, :]).astype(BF)
-    cross = pltpu.make_async_remote_copy(
-        src_ref=xsend, dst_ref=xrecv, send_sem=x_sem.at[0], recv_sem=x_sem.at[1],
-        device_id={"src": me, "xl": (my_y * 2 + 1 - hi) * 2 + c}, device_id_type=MESH)
-    cross.start()
-    for z in range(2):
-        ck[pl.ds(z * 128, 128), :] = cown[z, mine, :] + precv[z, mine, :]
-    cross.wait()
-    for z in range(2):
-        ck[pl.ds(z * 128, 128), :] += xrecv[z].astype(F32)
+        ck[pl.ds(z * 256, 256), :] = cown[z] + precv[z]
 
     halves = []
     for z in range(2):
-        v = jnp.concatenate([ck[pl.ds(z * 128 + sp, 8, stride=16), :] for sp in range(16)], axis=0)
+        v = jnp.concatenate([ck[pl.ds(z * 256 + sp, 16, stride=16), :] for sp in range(16)], axis=0)
         for b in range(4):
             step = 8 << b
-            v = v.reshape(8 >> b, 2, 8 << b, 128)
-            low, high = v[:, 0].reshape(64, 128), v[:, 1].reshape(64, 128)
-            keep = lane_bit((64, 128), b + 3)
+            v = v.reshape(8 >> b, 2, 16 << b, 128)
+            low, high = v[:, 0].reshape(128, 128), v[:, 1].reshape(128, 128)
+            keep = lane_bit((128, 128), b + 3)
             new_low = jnp.where(keep, low, pltpu.roll(high, step, 1))
             new_high = jnp.where(keep, pltpu.roll(low, 128 - step, 1), high)
-            parts = (8 >> b, 1, 8 << b, 128)
-            v = jnp.concatenate([new_low.reshape(parts), new_high.reshape(parts)], axis=1).reshape(128, 128)
-        halves.append(v.reshape(16, 8, 128))
+            parts = (8 >> b, 1, 16 << b, 128)
+            v = jnp.concatenate([new_low.reshape(parts), new_high.reshape(parts)], axis=1).reshape(256, 128)
+        halves.append(v.reshape(16, 16, 128))
     d_buf[...] = jnp.concatenate(halves, axis=1).astype(BF)
 
     def c1(k, to, frm):
@@ -224,11 +224,10 @@
     e_buf[m] = d_buf[m]
     lax.fori_loop(1, nm, c1_wait, 0)
 
-    for half in range(2):
-        for y in range(ny):
-            tile = e_buf[2 * y + half].astype(F32)
-            t_buf[pl.ds(half * 128 + y, 8, stride=16), :] = tile[:8]
-            t_buf[pl.ds(half * 128 + 8 + y, 8, stride=16), :] = tile[8:]
+    for y in range(ny):
+        tile = e_buf[2 * y].astype(F32) + e_buf[2 * y + 1].astype(F32)
+        t_buf[pl.ds(y, 16, stride=16), :] = tile[:16]
+        t_buf[pl.ds(8 + y, 16, stride=16), :] = tile[16:]
     h_buf[...] = t_buf[...].reshape(16, 16, 128).astype(BF)
 
     def c2(k, to, frm):
@@ -289,15 +288,13 @@
             pltpu.VMEM((2, 256, 128), F32),
             pltpu.VMEM((2, 256, 128), F32),
             pltpu.VMEM((2, 256, 128), F32),
-            pltpu.VMEM((2, 128, 128), BF),
-            pltpu.VMEM((2, 128, 128), BF),
+            pltpu.VMEM((512, 128), F32),
+            pltpu.VMEM((16, 32, 128), BF),
+            pltpu.VMEM((16, 32, 128), BF),
             pltpu.VMEM((256, 128), F32),
             pltpu.VMEM((16, 16, 128), BF),
             pltpu.VMEM((16, 16, 128), BF),
-            pltpu.VMEM((256, 128), F32),
-            pltpu.VMEM((16, 16, 128), BF),
-            pltpu.VMEM((16, 16, 128), BF),
-            dma((11,)), dma, dma((ns,)), dma((2,)), dma((2,)),
+            dma((11,)), dma, dma((ns,)), dma((2,)),
             dma((nm,)), dma((nm,)), dma((ns,)), dma((ns,)), pltpu.SemaphoreType.REGULAR,
         ],
         compiler_params=pltpu.CompilerParams(

time: 56.9 us -> 54.5 us (0.958)
  Pallas kernels: 54.4 us -> 52.1 us
    pallas_call x1, Pallas kernels: 54.4 us -> 52.1 us  [per_device(): pl.pallas_call(functools.partial(kernel, ns, ny, scale), out_shape=out_sh...]
where the time goes in v5:
time: 54.5 us; the launch traced here: 53.6 us
  Pallas kernels  52.1 us (96%)
  local copies, waits for them, and re-layouts  1.57 us (3%)
    pallas_call x1, Pallas kernels, per_device(): pl.pallas_call(functools.partial(kernel, ns, ny, scale), out_shape=out_sh...  52.1 us
    unnamed x1, local copies, waits for them, and re-layouts  1.57 us

profile of v5, /device:TPU:1, one launch (start us, length us, event | category | flops | bytes accessed | tf_op | source)
XLA Modules:
  0.0 53.6 jit_solution(7716325230208058914)
XLA Ops:
  0.0 52.1 %shard_map.46 = f32[16,8,256]{2,1,0:T(8,128)} custom-call(f32[512,1024]{1,0:T(8,128)} %bitcast.2, f32[512,1024]{1,0:T(8,128)} %bitcast.3, bf16[256,1024]{1,0:T(8,128)(2,1)} %constant.4.clone.thi_ref, bf16[256,1024]{1,0:T(8,128)(2,1)} %constant.5.clone.tlo_ref), custom_call_target="tpu_custom_call" | custom-call | tf_op jit(solution)/shard_map/pallas_call | solution.py:271
  52.1 1.6 %copy.6 = f32[16,8,256]{2,1,0:T(8,128)} copy(f32[16,8,256]{2,1,0:T(8,128)} %shard_map.46) | data formatting | bytes 262144

commit v6 on v5

--- a/solution.py
+++ b/solution.py
@@ -128,31 +128,33 @@
     for k in range(ns):
         s_buf[k] = u[k * 128:(k + 1) * 128, :].astype(BF).reshape(8, 16, 128)
 
-    def send(to, to_y):
+    z, x_lo = me // 2, me % 2
+    sign = 1 - 2 * c
+
+    def send(dz, t, x):
+        dy = 4 + (t + 1) // 2 * (1 - t % 2 * 2)
+        to = (z + sign * dz + ns) % (ns // 2) * 2 + (x_lo + x) % 2
+        to_y = (my_y + sign * dy + ns) % ny
         pltpu.make_async_remote_copy(
             src_ref=s_buf.at[to, to_y], dst_ref=r2.at[me, my_y], send_sem=s_send, recv_sem=s_recv.at[me],
             device_id={"src": to, "xl": to_y * Q + q}, device_id_type=MESH).start()
 
-    def go_column(k, carry):
-        send((me + k) % ns, my_y)
-        return carry
-
-    def go_row(k, carry):
-        send(me, (my_y + k) % ny)
-        return carry
-
-    def go(k, carry):
-        order = k * 37 % ((ns - 1) * (ny - 1))
-        send((me + 1 + order // (ny - 1)) % ns, (my_y + 1 + order % (ny - 1)) % ny)
-        return carry
-
-    lax.fori_loop(1, ny, go_row, 0)
-    lax.fori_loop(1, ns, go_column, 0)
+    def one(dz, k, carry):
+        send(dz, k // 2, 1 - k % 2)
+        return carry
+
+    def both(dz, k, carry):
+        send(dz * (1 - k % 2 * 2), k // 4, k // 2 % 2)
+        return carry
+
     pl.semaphore_wait(ready, ns - 1)
-    lax.fori_loop(0, (ns - 1) * (ny - 1), go, 0)
+    lax.fori_loop(0, 16, functools.partial(one, 4), 0)
+    for dz in (3, 2, 1):
+        lax.fori_loop(0, 32, functools.partial(both, dz), 0)
+    lax.fori_loop(0, 15, functools.partial(one, 0), 0)
     pltpu.make_async_copy(s_buf.at[me, my_y], r2.at[me, my_y], s_recv.at[me]).start()
 
-    def arrange(i2, carry):
+    def arrange(i2):
         top = lane_bit((16, 128), 6)
         real = lane_bit((16, 128), 5)
         for e in range(2):
@@ -171,9 +173,13 @@
                 bb[ra, pl.ds(at, 16), p * 128:(p + 1) * 128] = jnp.where(real, rows, -rows).astype(BF)
                 swapped = jnp.where(real, pltpu.roll(rows, 96, 1), pltpu.roll(rows, 32, 1))
                 bb[ra, pl.ds(128 + at, 16), p * 128:(p + 1) * 128] = swapped.astype(BF)
-        return carry
-
-    lax.fori_loop(0, ns // 2, arrange, 0)
+
+    def arrange_next(k, carry):
+        dz = 4 - (k + 1) // 2
+        arrange((z - sign * dz * (k % 2 * 2 - 1) + ns) % (ns // 2))
+        return carry
+
+    lax.fori_loop(0, ns // 2, arrange_next, 0)
     for part in (s_buf.at[pl.ds(0, ns - 1)], s_buf.at[0, pl.ds(0, ny - 1)]):
         pltpu.make_async_copy(part, part, s_send).wait()
 

time: 54.5 us -> 53.7 us (0.985)
  Pallas kernels: 52.1 us -> 51.5 us
where the time goes in v6:
time: 53.7 us; the launch traced here: 53.1 us
  Pallas kernels  51.5 us (96%)
  local copies, waits for them, and re-layouts  1.57 us (3%)
    pallas_call x1, Pallas kernels, per_device(): pl.pallas_call(functools.partial(kernel, ns, ny, scale), out_shape=out_sh...  51.5 us
    unnamed x1, local copies, waits for them, and re-layouts  1.57 us

profile of v6, /device:TPU:1, one launch (start us, length us, event | category | flops | bytes accessed | tf_op | source)
XLA Modules:
  0.0 53.1 jit_solution(2690063538299894022)
XLA Ops:
  0.0 51.5 %shard_map.46 = f32[16,8,256]{2,1,0:T(8,128)} custom-call(f32[512,1024]{1,0:T(8,128)} %bitcast.2, f32[512,1024]{1,0:T(8,128)} %bitcast.3, bf16[256,1024]{1,0:T(8,128)(2,1)} %constant.4.clone.thi_ref, bf16[256,1024]{1,0:T(8,128)(2,1)} %constant.5.clone.tlo_ref), custom_call_target="tpu_custom_call" | custom-call | tf_op jit(solution)/shard_map/pallas_call | solution.py:277
  51.5 1.6 %copy.6 = f32[16,8,256]{2,1,0:T(8,128)} copy(f32[16,8,256]{2,1,0:T(8,128)} %shard_map.46) | data formatting | bytes 262144

commit v7 on v6

--- a/solution.py
+++ b/solution.py
@@ -31,6 +31,10 @@
 
 def dot_nt(a, b):
     return lax.dot_general(a, b, NT, preferred_element_type=F32)
+
+
+def far_first(count, t):
+    return count // 2 + (t + 1) // 2 * (1 - t % 2 * 2)
 
 
 def lane_bit(shape, bit):
@@ -63,24 +67,27 @@
     barrier = pltpu.get_barrier_semaphore()
 
     def greet_src(k, carry):
-        pl.semaphore_signal(barrier, inc=1, device_id={"src": (me + k) % ns, "xl": j}, device_id_type=MESH)
+        to = (me + far_first(ns, k)) % ns
+        pl.semaphore_signal(barrier, inc=1, device_id={"src": to, "xl": j}, device_id_type=MESH)
         return carry
 
     def greet_y(k, carry):
-        pl.semaphore_signal(barrier, inc=1, device_id={"src": me, "xl": (my_y + k) % ny * Q + q}, device_id_type=MESH)
+        to = (my_y + far_first(ny, k)) % ny
+        pl.semaphore_signal(barrier, inc=1, device_id={"src": me, "xl": to * Q + q}, device_id_type=MESH)
         return carry
 
     def row_ready(k, carry):
-        pl.semaphore_signal(ready, inc=1, device_id={"src": (me + k) % ns, "xl": j}, device_id_type=MESH)
+        pl.semaphore_signal(ready, inc=1, device_id={"src": (me + far_first(ns, k)) % ns, "xl": j}, device_id_type=MESH)
         return carry
 
     def greet_x(k, carry):
-        pl.semaphore_signal(barrier, inc=1, device_id={"src": me, "xl": k * Q + (1 - hi) * 2 + c}, device_id_type=MESH)
-        return carry
-
-    lax.fori_loop(1, ns, greet_src, 0)
-    lax.fori_loop(1, ny, greet_y, 0)
+        to = (my_y + far_first(ny, k)) % ny
+        pl.semaphore_signal(barrier, inc=1, device_id={"src": me, "xl": to * Q + (1 - hi) * 2 + c}, device_id_type=MESH)
+        return carry
+
+    lax.fori_loop(0, ns - 1, greet_src, 0)
     lax.fori_loop(0, ny, greet_x, 0)
+    lax.fori_loop(0, ny - 1, greet_y, 0)
     pl.semaphore_signal(barrier, inc=1, device_id={"src": me, "xl": m * 2 + 1 - c}, device_id_type=MESH)
 
     for item in loads:
@@ -118,7 +125,7 @@
 
     lax.fori_loop(0, 8, split_a, 0)
     pl.semaphore_wait(barrier, ns + 2 * ny - 1)
-    lax.fori_loop(1, ns, row_ready, 0)
+    lax.fori_loop(0, ns - 1, row_ready, 0)
     lax.fori_loop(0, 2, transform, 0)
     for item in rec_loads:
         item.wait()
@@ -180,8 +187,6 @@
         return carry
 
     lax.fori_loop(0, ns // 2, arrange_next, 0)
-    for part in (s_buf.at[pl.ds(0, ns - 1)], s_buf.at[0, pl.ds(0, ny - 1)]):
-        pltpu.make_async_copy(part, part, s_send).wait()
 
     prod = dot_nt(acat[...], bb[1 - c])
     psend[0] = prod[:, :128]
@@ -219,14 +224,15 @@
             device_id={"src": me, "xl": to * 2 + c}, device_id_type=MESH)
 
     def c1_go(k, carry):
-        c1(k, (m + k) % nm, m).start()
+        d = far_first(nm, k)
+        c1(d, (m + d) % nm, m).start()
         return carry
 
     def c1_wait(k, carry):
         c1(k, (m + k) % nm, (m + nm - k) % nm).wait()
         return carry
 
-    lax.fori_loop(1, nm, c1_go, 0)
+    lax.fori_loop(0, nm - 1, c1_go, 0)
     e_buf[m] = d_buf[m]
     lax.fori_loop(1, nm, c1_wait, 0)
 
@@ -242,16 +248,20 @@
             device_id={"src": to, "xl": j}, device_id_type=MESH)
 
     def c2_go(k, carry):
-        c2(k, (me + k) % ns, me).start()
+        d = far_first(ns, k)
+        c2(d, (me + d) % ns, me).start()
         return carry
 
     def c2_wait(k, carry):
         c2(k, (me + k) % ns, (me + ns - k) % ns).wait()
         return carry
 
-    lax.fori_loop(1, ns, c2_go, 0)
+    lax.fori_loop(0, ns - 1, c2_go, 0)
     g_buf[me] = h_buf[me]
     lax.fori_loop(1, ns, c2_wait, 0)
+
+    for part in (s_buf.at[pl.ds(0, ns - 1)], s_buf.at[0, pl.ds(0, ny - 1)]):
+        pltpu.make_async_copy(part, part, s_send).wait()
 
     got = g_buf[...].astype(F32)
     for z in range(2):

time: 53.7 us -> 53.2 us (level)
  no operation moved by 1% of the time
where the time goes in v7:
time: 53.2 us; the launch traced here: 53 us
  Pallas kernels  51.4 us (97%)
  local copies, waits for them, and re-layouts  1.57 us (3%)
    pallas_call x1, Pallas kernels, per_device(): pl.pallas_call(functools.partial(kernel, ns, ny, scale), out_shape=out_sh...  51.4 us
    unnamed x1, local copies, waits for them, and re-layouts  1.57 us

profile of v7, /device:TPU:1, one launch (start us, length us, event | category | flops | bytes accessed | tf_op | source)
XLA Modules:
  0.0 53.0 jit_solution(15145244137339115811)
XLA Ops:
  0.0 51.4 %shard_map.46 = f32[16,8,256]{2,1,0:T(8,128)} custom-call(f32[512,1024]{1,0:T(8,128)} %bitcast.2, f32[512,1024]{1,0:T(8,128)} %bitcast.3, bf16[256,1024]{1,0:T(8,128)(2,1)} %constant.4.clone.thi_ref, bf16[256,1024]{1,0:T(8,128)(2,1)} %constant.5.clone.tlo_ref), custom_call_target="tpu_custom_call" | custom-call | tf_op jit(solution)/shard_map/pallas_call | solution.py:287
  51.4 1.6 %copy.6 = f32[16,8,256]{2,1,0:T(8,128)} copy(f32[16,8,256]{2,1,0:T(8,128)} %shard_map.46) | data formatting | bytes 262144

commit v8 on v7

--- a/solution.py
+++ b/solution.py
@@ -124,9 +124,9 @@
         return carry
 
     lax.fori_loop(0, 8, split_a, 0)
+    lax.fori_loop(0, 2, transform, 0)
     pl.semaphore_wait(barrier, ns + 2 * ny - 1)
     lax.fori_loop(0, ns - 1, row_ready, 0)
-    lax.fori_loop(0, 2, transform, 0)
     for item in rec_loads:
         item.wait()
     lax.fori_loop(0, 16, split_b, 0)
@@ -154,11 +154,29 @@
         send(dz * (1 - k % 2 * 2), k // 4, k // 2 % 2)
         return carry
 
+    def in_column(dz, k, carry):
+        send(dz * (1 - k % 2 * 2), ny - 1, k // 2 % 2)
+        return carry
+
+    def in_row(t, carry):
+        send(0, t, 0)
+        return carry
+
+    def beside(t, carry):
+        send(0, t, 1)
+        return carry
+
+    for k in range(2):
+        send(4, ny - 1, k)
+    for dz in (3, 2, 1):
+        lax.fori_loop(0, 4, functools.partial(in_column, dz), 0)
+    send(0, ny - 1, 1)
+    lax.fori_loop(0, ny - 1, in_row, 0)
     pl.semaphore_wait(ready, ns - 1)
-    lax.fori_loop(0, 16, functools.partial(one, 4), 0)
+    lax.fori_loop(0, 14, functools.partial(one, 4), 0)
     for dz in (3, 2, 1):
-        lax.fori_loop(0, 32, functools.partial(both, dz), 0)
-    lax.fori_loop(0, 15, functools.partial(one, 0), 0)
+        lax.fori_loop(0, 28, functools.partial(both, dz), 0)
+    lax.fori_loop(0, ny - 1, beside, 0)
     pltpu.make_async_copy(s_buf.at[me, my_y], r2.at[me, my_y], s_recv.at[me]).start()
 
     def arrange(i2):

time: 53.2 us -> 51 us (0.959)
  Pallas kernels: 51.4 us -> 49.3 us
    pallas_call x1, Pallas kernels: 51.4 us -> 49.3 us  [per_device(): pl.pallas_call(functools.partial(kernel, ns, ny, scale), out_shape=out_sh...]
where the time goes in v8:
time: 51 us; the launch traced here: 50.9 us
  Pallas kernels  49.3 us (97%)
  local copies, waits for them, and re-layouts  1.57 us (3%)
    pallas_call x1, Pallas kernels, per_device(): pl.pallas_call(functools.partial(kernel, ns, ny, scale), out_shape=out_sh...  49.3 us
    unnamed x1, local copies, waits for them, and re-layouts  1.57 us

profile of v8, /device:TPU:1, one launch (start us, length us, event | category | flops | bytes accessed | tf_op | source)
XLA Modules:
  0.0 50.9 jit_solution(8789962468032052920)
XLA Ops:
  0.0 49.3 %shard_map.46 = f32[16,8,256]{2,1,0:T(8,128)} custom-call(f32[512,1024]{1,0:T(8,128)} %bitcast.2, f32[512,1024]{1,0:T(8,128)} %bitcast.3, bf16[256,1024]{1,0:T(8,128)(2,1)} %constant.4.clone.thi_ref, bf16[256,1024]{1,0:T(8,128)(2,1)} %constant.5.clone.tlo_ref), custom_call_target="tpu_custom_call" | custom-call | tf_op jit(solution)/shard_map/pallas_call | solution.py:305
  49.3 1.6 %copy.6 = f32[16,8,256]{2,1,0:T(8,128)} copy(f32[16,8,256]{2,1,0:T(8,128)} %shard_map.46) | data formatting | bytes 262144

commit v9 on v8

--- a/solution.py
+++ b/solution.py
@@ -125,11 +125,11 @@
 
     lax.fori_loop(0, 8, split_a, 0)
     lax.fori_loop(0, 2, transform, 0)
-    pl.semaphore_wait(barrier, ns + 2 * ny - 1)
-    lax.fori_loop(0, ns - 1, row_ready, 0)
     for item in rec_loads:
         item.wait()
     lax.fori_loop(0, 16, split_b, 0)
+    pl.semaphore_wait(barrier, ns + 2 * ny - 1)
+    lax.fori_loop(0, ns - 1, row_ready, 0)
     lax.fori_loop(2, 4, transform, 0)
 
     for k in range(ns):

time: 51 us -> 51.4 us (level)
  no operation moved by 1% of the time
where the time goes in v9:
time: 51.4 us; the launch traced here: 51.1 us
  Pallas kernels  49.5 us (96%)
  local copies, waits for them, and re-layouts  1.57 us (3%)
    pallas_call x1, Pallas kernels, per_device(): pl.pallas_call(functools.partial(kernel, ns, ny, scale), out_shape=out_sh...  49.5 us
    unnamed x1, local copies, waits for them, and re-layouts  1.57 us

profile of v9, /device:TPU:1, one launch (start us, length us, event | category | flops | bytes accessed | tf_op | source)
XLA Modules:
  0.0 51.1 jit_solution(3317366243479220983)
XLA Ops:
  0.0 49.5 %shard_map.46 = f32[16,8,256]{2,1,0:T(8,128)} custom-call(f32[512,1024]{1,0:T(8,128)} %bitcast.2, f32[512,1024]{1,0:T(8,128)} %bitcast.3, bf16[256,1024]{1,0:T(8,128)(2,1)} %constant.4.clone.thi_ref, bf16[256,1024]{1,0:T(8,128)(2,1)} %constant.5.clone.tlo_ref), custom_call_target="tpu_custom_call" | custom-call | tf_op jit(solution)/shard_map/pallas_call | solution.py:305
  49.5 1.6 %copy.6 = f32[16,8,256]{2,1,0:T(8,128)} copy(f32[16,8,256]{2,1,0:T(8,128)} %shard_map.46) | data formatting | bytes 262144
